TPU v7x, 256 devices: a whole 4x4x8 slice. The times are simulated.
256 devices in a mesh: dom: 64 (over z, y, core), chan: 4 (over x).
Axes of the slice: x: 4, y: 4, z: 8, core: 2. Of those that a mesh axis runs over, the one named last changes fastest.
Arguments:
- features: bfloat16 [256, 65536], P('chan', 'dom'), may hold values from -6 to 6
- cotangent: bfloat16 [256, 65536], P('chan', 'dom'), may hold values from -6 to 6
- weights: bfloat16 [9, 256, 256], P(None, 'chan'), may hold values from -0.375 to 0.375
- tile_values: float32 [4096, 128, 128], P('dom'), may hold values from -0.046875 to 0.046875
- tile_cols: int32 [64, 8, 8], P('dom'), may hold values from 0 to 11, as said below
- send_list: int32 [64, 4, 128], P('dom'), may hold values from 0 to 1023
Outputs:
- input_grad: float32 [256, 65536], P('chan', 'dom')
- weight_grad: float32 [9, 256, 256], P(None, None, 'chan')
Inputs may be any that keep to these rules, and one draw needn't show every extreme that they name: `tile_cols`: values below 8 are blocks of the partition's own nodes; 8 + s is the block received from neighbour slot s. Tile 0 of row block r has column block r.
All inputs are finite; a program needn't handle non-finite values.
Results may differ from a plain program's by a relative error of at most 0.0003.
Values may be sent and summed in bfloat16 or wider, within the bound.
A program may use at most 128 MiB of HBM per device.

v0:
```python
import jax
import jax.numpy as jnp
from jax import lax
from jax.sharding import PartitionSpec as P

NEIGHBOUR_SHIFTS = (1, -1, 2, -2)


def from_behind(block, axis, distance):
    devices = range(lax.axis_size(axis))
    route = [((i - distance) % len(devices), i) for i in devices]
    return lax.ppermute(block, axis, route)


def exchange_rows(outgoing):
    received = [
        from_behind(outgoing[:, slot_index], "dom", offset)
        for slot_index, offset in enumerate(NEIGHBOUR_SHIFTS)
    ]
    return received


def apply_operator(field_in, tile_values, tile_cols, send_list):
    channels, local_nodes = field_in.shape
    tile_size = tile_values.shape[-1]
    per_row = tile_cols.shape[-1]
    outgoing = jnp.take(field_in, send_list[0], axis=1)
    received = exchange_rows(outgoing)
    extended = jnp.concatenate([field_in] + received, axis=1)
    blocks = extended.reshape(channels, -1, tile_size)
    picked = jnp.take(blocks, tile_cols.reshape(-1), axis=1)
    product = jnp.einsum("ctj,tjk->ctk", picked, tile_values, precision=lax.Precision.HIGHEST)
    return (
        product.reshape(channels, -1, per_row, tile_size).sum(axis=2).reshape(channels, local_nodes)
    )


def local(features, cotangent, weights, tile_values, tile_cols, send_list):
    top_order = weights.shape[0] - 1
    local_nodes = features.shape[1]

    def operator_on(field_in):
        return apply_operator(field_in, tile_values, tile_cols, send_list)

    feat_all, cot_all = (
        lax.all_gather(features, "chan", axis=0, tiled=True),
        lax.all_gather(cotangent, "chan", axis=0, tiled=True),
    )
    feat_wide = feat_all.astype(jnp.float32)

    def mixed_term(order_index):
        return jnp.dot(weights[order_index], cot_all, preferred_element_type=jnp.float32)

    def grad_term(state):
        return lax.dot_general(
            feat_wide, state, (((1,), (1,)), ((), ())), precision=lax.Precision.HIGHEST
        )

    cheb_prev = cotangent.astype(jnp.float32)
    grad_terms = [grad_term(cheb_prev)]
    cheb_now = operator_on(cheb_prev)
    grad_terms.append(grad_term(cheb_now))
    for order_index in range(2, top_order + 1):
        cheb_prev, cheb_now = (cheb_now, 2.0 * operator_on(cheb_now) - cheb_prev)
        grad_terms.append(grad_term(cheb_now))
    current = mixed_term(top_order)
    clen_later = jnp.zeros_like(current)
    for order_index in range(top_order - 1, 0, -1):
        current, clen_later = (
            mixed_term(order_index) + 2.0 * operator_on(current) - clen_later,
            current,
        )
    input_grad = mixed_term(0) + operator_on(current) - clen_later
    local_grads = jnp.stack(grad_terms)
    summed = lax.psum(local_grads, "dom")
    nodes_all = lax.axis_size("dom") * local_nodes
    return (input_grad, summed * float(nodes_all) ** (-0.5))


def solution(mesh):
    placed = (
        P("chan", "dom"),
        P("chan", "dom"),
        P(None, "chan", None),
        P("dom", None, None),
        P("dom", None, None),
        P("dom", None, None),
    )
    return jax.shard_map(
        local,
        mesh=mesh,
        in_specs=placed,
        out_specs=(P("chan", "dom"), P(None, None, "chan")),
        check_vma=False,
    )
```

profile of v0, /device:TPU:1, one launch (start us, length us, event | category | flops | bytes accessed | tf_op | source)
XLA Modules:
  0.0 663.6 jit_solution(9862079954037837758)
XLA Ops:
  8.6 12.5 %all_gather.6 = bf16[256,1024]{1,0:T(8,128)(2,1)S(1)} all-gather(bf16[64,1024]{1,0:T(8,128)(2,1)} %param.11), channel_id=1, replica_groups=mesh['dom'=64,'chan'=4] {'chan'}, dimensions={0}, use_global_device_ids=true | all-gather | bytes 655360 | tf_op jit(solution)/shard_map/all_gather | solution.py:47
  25.0 3.5 collective-permute-start
  29.8 5.6 collective-permute-start.3
  37.7 10.2 %all_gather.7 = bf16[256,1024]{1,0:T(8,128)(2,1)S(1)} all-gather(bf16[64,1024]{1,0:T(8,128)(2,1)S(1)} %copy-done.13), channel_id=1, replica_groups=mesh['dom'=64,'chan'=4] {'chan'}, dimensions={0}, use_global_device_ids=true | all-gather | bytes 655360 | tf_op jit(solution)/shard_map/all_gather | solution.py:46
  48.8 6.3 collective-permute-start.33
  56.0 11.5 %collective-permute-done.34 = f32[64,128]{0,1:T(8,128)S(1)} collective-permute-done((f32[64,128]{0,1:T(8,128)S(1)}, f32[64,128]{0,1:T(8,128)S(1)}, u32[]{:S(2)}, u32[]{:S(2)}) %collective-permute-start.34) | collective-permute-done | bytes 32800 | tf_op jit(solution)/shard_map/ppermute | solution.py:12
  68.7 2.2 collective-permute-done.35
  71.8 6.4 bitcast_reduce_fusion.7
  87.8 2.0 gather_fusion.1
  89.8 6.7 %bitcast_reduce_fusion.15 = f32[64,8,128]{2,0,1:T(8,128)S(1)} fusion(f32[64,128,128]{2,1,0:T(8,128)} %param.13, f32[64,64,128]{2,1,0:T(8,128)} %gather_fusion.1, pred[64]{0:T(512)(128)(4,1)S(1)} %compare_and_fusion), kind=kOutput, calls=%fused_computation.47 | convolution fusion | flops 806289408 | bytes 6553664 | tf_op jit(solution)/shard_map/ctj,tjk->ctk/dot_general | solution.py:32
  101.1 4.8 collective-permute-start.7
  109.7 4.2 collective-permute-start.37
  114.0 4.8 collective-permute-start.39
  118.9 2.0 gather_fusion.3
  120.9 6.7 %bitcast_reduce_fusion.14 = f32[64,8,128]{2,0,1:T(8,128)S(1)} fusion(f32[64,128,128]{2,1,0:T(8,128)} %param.13, f32[64,64,128]{2,1,0:T(8,128)} %gather_fusion.3, pred[64]{0:T(512)(128)(4,1)S(1)} %compare_and_fusion), kind=kOutput, calls=%fused_computation.46 | convolution fusion | flops 806289408 | bytes 6553664 | tf_op jit(solution)/shard_map/ctj,tjk->ctk/dot_general | solution.py:32
  132.6 3.7 collective-permute-start.9
  139.2 4.9 collective-permute-start.11
  148.4 2.0 gather_fusion.19
  150.5 6.7 %bitcast_reduce_fusion.6 = f32[64,8,128]{2,0,1:T(8,128)S(1)} fusion(f32[64,128,128]{2,1,0:T(8,128)} %param.13, f32[64,64,128]{2,1,0:T(8,128)} %gather_fusion.19, pred[64]{0:T(512)(128)(4,1)S(1)} %compare_and_fusion), kind=kOutput, calls=%fused_computation.38 | convolution fusion | flops 806289408 | bytes 6553664 | tf_op jit(solution)/shard_map/ctj,tjk->ctk/dot_general | solution.py:32
  166.7 3.8 collective-permute-start.41
  170.5 5.0 collective-permute-start.43
  175.6 2.0 gather_fusion.5
  177.6 6.7 %bitcast_reduce_fusion.13 = f32[64,8,128]{2,0,1:T(8,128)S(1)} fusion(f32[64,128,128]{2,1,0:T(8,128)} %param.13, f32[64,64,128]{2,1,0:T(8,128)} %gather_fusion.5, pred[64]{0:T(512)(128)(4,1)S(1)} %compare_and_fusion), kind=kOutput, calls=%fused_computation.45 | convolution fusion | flops 806289408 | bytes 6553664 | tf_op jit(solution)/shard_map/ctj,tjk->ctk/dot_general | solution.py:32
  189.9 3.7 collective-permute-start.13
  196.5 5.0 collective-permute-start.15
  205.8 2.0 gather_fusion.21
  207.8 6.7 %bitcast_reduce_fusion.5 = f32[64,8,128]{2,0,1:T(8,128)S(1)} fusion(f32[64,128,128]{2,1,0:T(8,128)} %param.13, f32[64,64,128]{2,1,0:T(8,128)} %gather_fusion.21, pred[64]{0:T(512)(128)(4,1)S(1)} %compare_and_fusion), kind=kOutput, calls=%fused_computation.37 | convolution fusion | flops 806289408 | bytes 6553664 | tf_op jit(solution)/shard_map/ctj,tjk->ctk/dot_general | solution.py:32
  222.5 3.8 collective-permute-start.45
  228.9 5.2 collective-permute-start.47
  237.9 2.0 gather_fusion.7
  240.0 6.7 %bitcast_reduce_fusion.12 = f32[64,8,128]{2,0,1:T(8,128)S(1)} fusion(f32[64,128,128]{2,1,0:T(8,128)} %param.13, f32[64,64,128]{2,1,0:T(8,128)} %gather_fusion.7, pred[64]{0:T(512)(128)(4,1)S(1)} %compare_and_fusion), kind=kOutput, calls=%fused_computation.44 | convolution fusion | flops 806289408 | bytes 6553664 | tf_op jit(solution)/shard_map/ctj,tjk->ctk/dot_general | solution.py:32
  252.2 3.8 collective-permute-start.17
  258.1 4.9 collective-permute-start.19
  266.5 2.0 gather_fusion.23
  268.6 6.7 %bitcast_reduce_fusion.4 = f32[64,8,128]{2,0,1:T(8,128)S(1)} fusion(f32[64,128,128]{2,1,0:T(8,128)} %param.13, f32[64,64,128]{2,1,0:T(8,128)} %gather_fusion.23, pred[64]{0:T(512)(128)(4,1)S(1)} %compare_and_fusion), kind=kOutput, calls=%fused_computation.36 | convolution fusion | flops 806289408 | bytes 6553664 | tf_op jit(solution)/shard_map/ctj,tjk->ctk/dot_general | solution.py:32
  281.3 3.8 collective-permute-start.49
  286.6 5.0 collective-permute-start.51
  293.2 2.0 gather_fusion.9
  295.2 6.7 %bitcast_reduce_fusion.11 = f32[64,8,128]{2,0,1:T(8,128)S(1)} fusion(f32[64,128,128]{2,1,0:T(8,128)} %param.13, f32[64,64,128]{2,1,0:T(8,128)} %gather_fusion.9, pred[64]{0:T(512)(128)(4,1)S(1)} %compare_and_fusion), kind=kOutput, calls=%fused_computation.43 | convolution fusion | flops 806289408 | bytes 6553664 | tf_op jit(solution)/shard_map/ctj,tjk->ctk/dot_general | solution.py:32
  306.9 3.8 collective-permute-start.21
  312.8 5.0 collective-permute-start.23
  321.3 2.0 gather_fusion.25
  323.4 6.7 %bitcast_reduce_fusion.3 = f32[64,8,128]{2,0,1:T(8,128)S(1)} fusion(f32[64,128,128]{2,1,0:T(8,128)} %param.13, f32[64,64,128]{2,1,0:T(8,128)} %gather_fusion.25, pred[64]{0:T(512)(128)(4,1)S(1)} %compare_and_fusion), kind=kOutput, calls=%fused_computation.35 | convolution fusion | flops 806289408 | bytes 6553664 | tf_op jit(solution)/shard_map/ctj,tjk->ctk/dot_general | solution.py:32
  336.1 3.8 collective-permute-start.53
  340.0 5.3 collective-permute-start.55
  345.3 2.0 gather_fusion.11
  347.3 6.7 %bitcast_reduce_fusion.10 = f32[64,8,128]{2,0,1:T(8,128)S(1)} fusion(f32[64,128,128]{2,1,0:T(8,128)} %param.13, f32[64,64,128]{2,1,0:T(8,128)} %gather_fusion.11, pred[64]{0:T(512)(128)(4,1)S(1)} %compare_and_fusion), kind=kOutput, calls=%fused_computation.42 | convolution fusion | flops 806289408 | bytes 6553664 | tf_op jit(solution)/shard_map/ctj,tjk->ctk/dot_general | solution.py:32
  359.7 3.7 collective-permute-start.25
  365.5 4.9 collective-permute-start.27
  373.9 2.0 gather_fusion.27
  375.9 6.7 %bitcast_reduce_fusion.2 = f32[64,8,128]{2,0,1:T(8,128)S(1)} fusion(f32[64,128,128]{2,1,0:T(8,128)} %param.13, f32[64,64,128]{2,1,0:T(8,128)} %gather_fusion.27, pred[64]{0:T(512)(128)(4,1)S(1)} %compare_and_fusion), kind=kOutput, calls=%fused_computation.34 | convolution fusion | flops 806289408 | bytes 6553664 | tf_op jit(solution)/shard_map/ctj,tjk->ctk/dot_general | solution.py:32
  388.7 3.8 collective-permute-start.57
  394.0 5.0 collective-permute-start.59
  400.5 2.0 gather_fusion.13
  402.6 6.7 %bitcast_reduce_fusion.9 = f32[64,8,128]{2,0,1:T(8,128)S(1)} fusion(f32[64,128,128]{2,1,0:T(8,128)} %param.13, f32[64,64,128]{2,1,0:T(8,128)} %gather_fusion.13, pred[64]{0:T(512)(128)(4,1)S(1)} %compare_and_fusion), kind=kOutput, calls=%fused_computation.41 | convolution fusion | flops 806289408 | bytes 6553664 | tf_op jit(solution)/shard_map/ctj,tjk->ctk/dot_general | solution.py:32
  414.9 3.8 collective-permute-start.29
  420.7 5.0 collective-permute-start.31
  431.3 6.7 %bitcast_reduce_fusion.1 = f32[64,8,128]{2,0,1:T(8,128)S(1)} fusion(f32[64,128,128]{2,1,0:T(8,128)} %param.13, f32[64,64,128]{2,1,0:T(8,128)} %gather_fusion.29, pred[64]{0:T(512)(128)(4,1)S(1)} %compare_and_fusion), kind=kOutput, calls=%fused_computation.33 | convolution fusion | flops 806289408 | bytes 6553664 | tf_op jit(solution)/shard_map/ctj,tjk->ctk/dot_general | solution.py:32
  443.4 3.8 collective-permute-start.61
  448.8 5.1 collective-permute-start.63
  461.3 2.1 gather_fusion.31
  463.4 6.7 %bitcast_reduce_fusion = f32[64,8,128]{2,0,1:T(8,128)S(1)} fusion(f32[64,128,128]{2,1,0:T(8,128)} %param.13, f32[64,64,128]{2,1,0:T(8,128)} %gather_fusion.31, pred[64]{0:T(512)(128)(4,1)S(1)} %compare_and_fusion), kind=kOutput, calls=%fused_computation.32 | convolution fusion | flops 806289408 | bytes 6553664 | tf_op jit(solution)/shard_map/ctj,tjk->ctk/dot_general | solution.py:32
  471.6 6.7 %bitcast_reduce_fusion.8 = f32[64,8,128]{2,0,1:T(8,128)S(1)} fusion(f32[64,128,128]{2,1,0:T(8,128)} %param.13, f32[64,64,128]{2,1,0:T(8,128)} %gather_fusion.15, pred[64]{0:T(512)(128)(4,1)S(1)} %compare_and_fusion), kind=kOutput, calls=%fused_computation.40 | convolution fusion | flops 806289408 | bytes 6553664 | tf_op jit(solution)/shard_map/ctj,tjk->ctk/dot_general | solution.py:32
  480.0 174.4 %all-reduce.2.cloned.1.call-done = f32[9,256,64]{1,2,0:T(8,128)} async-done(((f32[9,256,64]{1,2,0:T(8,128)}), f32[9,256,64]{1,2,0:T(8,128)}) %all-reduce.2.cloned.1.call-update) | async-done | bytes 589840 | tf_op jit(solution)/shard_map/psum | solution.py:75
  (328 shorter events, 169.3 us)
Async XLA Ops:
  7.2 647.2 %all-reduce.2.cloned.1.call-start = ((), (), s32[]{:S(2)}) async-start(), calls=%async_computation | async-start | bytes 1179648 | tf_op jit(solution)/shard_map/psum | solution.py:75
  25.0 55.2 %collective-permute-start = (f32[64,128]{1,0:T(8,128)}, f32[64,128]{1,0:T(8,128)}, u32[]{:S(2)}, u32[]{:S(2)}) collective-permute-start(f32[64,128]{1,0:T(8,128)} %get-tuple-element.67), channel_id=1, source_target_pairs={{252,0},{0,4},{4,8},{8,12},{12,16},{16,20},{20,24},{24,28},{28,32}... | collective-permute-start | bytes 98312 | tf_op jit(solution)/shard_map/ppermute | solution.py:12
  28.5 53.0 %collective-permute-start.1 = (f32[64,128]{1,0:T(8,128)}, f32[64,128]{1,0:T(8,128)}, u32[]{:S(2)}, u32[]{:S(2)}) collective-permute-start(f32[64,128]{1,0:T(8,128)} %get-tuple-element.66), channel_id=1, source_target_pairs={{4,0},{8,4},{12,8},{16,12},{20,16},{24,20},{28,24},{32,28},{36,32}... | collective-permute-start | bytes 98312 | tf_op jit(solution)/shard_map/ppermute | solution.py:12
  29.3 53.6 %collective-permute-start.2 = (f32[64,128]{1,0:T(8,128)}, f32[64,128]{1,0:T(8,128)}, u32[]{:S(2)}, u32[]{:S(2)}) collective-permute-start(f32[64,128]{1,0:T(8,128)} %get-tuple-element.65), channel_id=1, source_target_pairs={{248,0},{252,4},{0,8},{4,12},{8,16},{12,20},{16,24},{20,28},{24,32... | collective-permute-start | bytes 98312 | tf_op jit(solution)/shard_map/ppermute | solution.py:12
  29.8 55.6 %collective-permute-start.3 = (f32[64,128]{1,0:T(8,128)}, f32[64,128]{1,0:T(8,128)}, u32[]{:S(2)}, u32[]{:S(2)}) collective-permute-start(f32[64,128]{1,0:T(8,128)} %get-tuple-element.64), channel_id=1, source_target_pairs={{8,0},{12,4},{16,8},{20,12},{24,16},{28,20},{32,24},{36,28},{40,32... | collective-permute-start | bytes 98312 | tf_op jit(solution)/shard_map/ppermute | solution.py:12
  36.8 12.0 %collective-permute-start.32 = (f32[64,128]{0,1:T(8,128)S(1)}, f32[64,128]{0,1:T(8,128)S(1)}, u32[]{:S(2)}, u32[]{:S(2)}) collective-permute-start(f32[64,128]{0,1:T(8,128)S(1)} %get-tuple-element.35), channel_id=1, source_target_pairs={{252,0},{0,4},{4,8},{8,12},{12,16},{16,20},{20,24},{24,28},{28,32}... | collective-permute-start | bytes 98312 | tf_op jit(solution)/shard_map/ppermute | solution.py:12
  48.8 7.2 %collective-permute-start.33 = (f32[64,128]{0,1:T(8,128)S(1)}, f32[64,128]{0,1:T(8,128)S(1)}, u32[]{:S(2)}, u32[]{:S(2)}) collective-permute-start(f32[64,128]{0,1:T(8,128)S(1)} %get-tuple-element.34), channel_id=1, source_target_pairs={{4,0},{8,4},{12,8},{16,12},{20,16},{24,20},{28,24},{32,28},{36,32}... | collective-permute-start | bytes 98312 | tf_op jit(solution)/shard_map/ppermute | solution.py:12
  56.0 11.5 %collective-permute-start.34 = (f32[64,128]{0,1:T(8,128)S(1)}, f32[64,128]{0,1:T(8,128)S(1)}, u32[]{:S(2)}, u32[]{:S(2)}) collective-permute-start(f32[64,128]{0,1:T(8,128)S(1)} %get-tuple-element.33), channel_id=1, source_target_pairs={{248,0},{252,4},{0,8},{4,12},{8,16},{12,20},{16,24},{20,28},{24,32... | collective-permute-start | bytes 98312 | tf_op jit(solution)/shard_map/ppermute | solution.py:12
  98.9 10.9 %collective-permute-start.4 = (f32[64,128]{1,0:T(8,128)S(1)}, f32[64,128]{1,0:T(8,128)S(1)}, u32[]{:S(2)}, u32[]{:S(2)}) collective-permute-start(f32[64,128]{1,0:T(8,128)S(1)} %get-tuple-element.63), channel_id=1, source_target_pairs={{252,0},{0,4},{4,8},{8,12},{12,16},{16,20},{20,24},{24,28},{28,32}... | collective-permute-start | bytes 98312 | tf_op jit(solution)/shard_map/ppermute | solution.py:12
  100.2 13.7 %collective-permute-start.5 = (f32[64,128]{1,0:T(8,128)S(1)}, f32[64,128]{1,0:T(8,128)S(1)}, u32[]{:S(2)}, u32[]{:S(2)}) collective-permute-start(f32[64,128]{1,0:T(8,128)S(1)} %get-tuple-element.62), channel_id=1, source_target_pairs={{4,0},{8,4},{12,8},{16,12},{20,16},{24,20},{28,24},{32,28},{36,32}... | collective-permute-start | bytes 98312 | tf_op jit(solution)/shard_map/ppermute | solution.py:12
  101.1 12.9 %collective-permute-start.6 = (f32[64,128]{1,0:T(8,128)S(1)}, f32[64,128]{1,0:T(8,128)S(1)}, u32[]{:S(2)}, u32[]{:S(2)}) collective-permute-start(f32[64,128]{1,0:T(8,128)S(1)} %get-tuple-element.61), channel_id=1, source_target_pairs={{248,0},{252,4},{0,8},{4,12},{8,16},{12,20},{16,24},{20,28},{24,32... | collective-permute-start | bytes 98312 | tf_op jit(solution)/shard_map/ppermute | solution.py:12
  101.1 17.8 %collective-permute-start.7 = (f32[64,128]{1,0:T(8,128)S(1)}, f32[64,128]{1,0:T(8,128)S(1)}, u32[]{:S(2)}, u32[]{:S(2)}) collective-permute-start(f32[64,128]{1,0:T(8,128)S(1)} %get-tuple-element.60), channel_id=1, source_target_pairs={{8,0},{12,4},{16,8},{20,12},{24,16},{28,20},{32,24},{36,28},{40,32... | collective-permute-start | bytes 98312 | tf_op jit(solution)/shard_map/ppermute | solution.py:12
  107.9 24.7 %collective-permute-start.36 = (f32[64,128]{0,1:T(8,128)}, f32[64,128]{0,1:T(8,128)}, u32[]{:S(2)}, u32[]{:S(2)}) collective-permute-start(f32[64,128]{0,1:T(8,128)} %get-tuple-element.31), channel_id=1, source_target_pairs={{252,0},{0,4},{4,8},{8,12},{12,16},{16,20},{20,24},{24,28},{28,32}... | collective-permute-start | bytes 98312 | tf_op jit(solution)/shard_map/ppermute | solution.py:12
  109.7 28.0 %collective-permute-start.37 = (f32[64,128]{0,1:T(8,128)}, f32[64,128]{0,1:T(8,128)}, u32[]{:S(2)}, u32[]{:S(2)}) collective-permute-start(f32[64,128]{0,1:T(8,128)} %get-tuple-element.30), channel_id=1, source_target_pairs={{4,0},{8,4},{12,8},{16,12},{20,16},{24,20},{28,24},{32,28},{36,32}... | collective-permute-start | bytes 98312 | tf_op jit(solution)/shard_map/ppermute | solution.py:12
  113.9 25.2 %collective-permute-start.38 = (f32[64,128]{0,1:T(8,128)}, f32[64,128]{0,1:T(8,128)}, u32[]{:S(2)}, u32[]{:S(2)}) collective-permute-start(f32[64,128]{0,1:T(8,128)} %get-tuple-element.29), channel_id=1, source_target_pairs={{248,0},{252,4},{0,8},{4,12},{8,16},{12,20},{16,24},{20,28},{24,32... | collective-permute-start | bytes 98312 | tf_op jit(solution)/shard_map/ppermute | solution.py:12
  114.0 31.6 %collective-permute-start.39 = (f32[64,128]{0,1:T(8,128)}, f32[64,128]{0,1:T(8,128)}, u32[]{:S(2)}, u32[]{:S(2)}) collective-permute-start(f32[64,128]{0,1:T(8,128)} %get-tuple-element.28), channel_id=1, source_target_pairs={{8,0},{12,4},{16,8},{20,12},{24,16},{28,20},{32,24},{36,28},{40,32... | collective-permute-start | bytes 98312 | tf_op jit(solution)/shard_map/ppermute | solution.py:12
  130.7 36.0 %collective-permute-start.8 = (f32[64,128]{1,0:T(8,128)}, f32[64,128]{1,0:T(8,128)S(1)}, u32[]{:S(2)}, u32[]{:S(2)}) collective-permute-start(f32[64,128]{1,0:T(8,128)} %get-tuple-element.59), channel_id=1, source_target_pairs={{252,0},{0,4},{4,8},{8,12},{12,16},{16,20},{20,24},{24,28},{28,32}... | collective-permute-start | bytes 98312 | tf_op jit(solution)/shard_map/ppermute | solution.py:12
  132.6 37.9 %collective-permute-start.9 = (f32[64,128]{1,0:T(8,128)}, f32[64,128]{1,0:T(8,128)S(1)}, u32[]{:S(2)}, u32[]{:S(2)}) collective-permute-start(f32[64,128]{1,0:T(8,128)} %get-tuple-element.58), channel_id=1, source_target_pairs={{4,0},{8,4},{12,8},{16,12},{20,16},{24,20},{28,24},{32,28},{36,32}... | collective-permute-start | bytes 98312 | tf_op jit(solution)/shard_map/ppermute | solution.py:12
  137.7 32.7 %collective-permute-start.10 = (f32[64,128]{1,0:T(8,128)}, f32[64,128]{1,0:T(8,128)S(1)}, u32[]{:S(2)}, u32[]{:S(2)}) collective-permute-start(f32[64,128]{1,0:T(8,128)} %get-tuple-element.57), channel_id=1, source_target_pairs={{248,0},{252,4},{0,8},{4,12},{8,16},{12,20},{16,24},{20,28},{24,32... | collective-permute-start | bytes 98312 | tf_op jit(solution)/shard_map/ppermute | solution.py:12
  139.2 36.3 %collective-permute-start.11 = (f32[64,128]{1,0:T(8,128)}, f32[64,128]{1,0:T(8,128)S(1)}, u32[]{:S(2)}, u32[]{:S(2)}) collective-permute-start(f32[64,128]{1,0:T(8,128)} %get-tuple-element.56), channel_id=1, source_target_pairs={{8,0},{12,4},{16,8},{20,12},{24,16},{28,20},{32,24},{36,28},{40,32... | collective-permute-start | bytes 98312 | tf_op jit(solution)/shard_map/ppermute | solution.py:12
  164.8 25.1 %collective-permute-start.40 = (f32[64,128]{0,1:T(8,128)}, f32[64,128]{0,1:T(8,128)}, u32[]{:S(2)}, u32[]{:S(2)}) collective-permute-start(f32[64,128]{0,1:T(8,128)} %get-tuple-element.27), channel_id=1, source_target_pairs={{252,0},{0,4},{4,8},{8,12},{12,16},{16,20},{20,24},{24,28},{28,32}... | collective-permute-start | bytes 98312 | tf_op jit(solution)/shard_map/ppermute | solution.py:12
  166.7 28.4 %collective-permute-start.41 = (f32[64,128]{0,1:T(8,128)}, f32[64,128]{0,1:T(8,128)}, u32[]{:S(2)}, u32[]{:S(2)}) collective-permute-start(f32[64,128]{0,1:T(8,128)} %get-tuple-element.26), channel_id=1, source_target_pairs={{4,0},{8,4},{12,8},{16,12},{20,16},{24,20},{28,24},{32,28},{36,32}... | collective-permute-start | bytes 98312 | tf_op jit(solution)/shard_map/ppermute | solution.py:12
  170.4 26.0 %collective-permute-start.42 = (f32[64,128]{0,1:T(8,128)}, f32[64,128]{0,1:T(8,128)}, u32[]{:S(2)}, u32[]{:S(2)}) collective-permute-start(f32[64,128]{0,1:T(8,128)} %get-tuple-element.25), channel_id=1, source_target_pairs={{248,0},{252,4},{0,8},{4,12},{8,16},{12,20},{16,24},{20,28},{24,32... | collective-permute-start | bytes 98312 | tf_op jit(solution)/shard_map/ppermute | solution.py:12
  170.5 32.5 %collective-permute-start.43 = (f32[64,128]{0,1:T(8,128)}, f32[64,128]{0,1:T(8,128)}, u32[]{:S(2)}, u32[]{:S(2)}) collective-permute-start(f32[64,128]{0,1:T(8,128)} %get-tuple-element.24), channel_id=1, source_target_pairs={{8,0},{12,4},{16,8},{20,12},{24,16},{28,20},{32,24},{36,28},{40,32... | collective-permute-start | bytes 98312 | tf_op jit(solution)/shard_map/ppermute | solution.py:12
  188.0 34.5 %collective-permute-start.12 = (f32[64,128]{1,0:T(8,128)S(1)}, f32[64,128]{1,0:T(8,128)S(1)}, u32[]{:S(2)}, u32[]{:S(2)}) collective-permute-start(f32[64,128]{1,0:T(8,128)S(1)} %get-tuple-element.55), channel_id=1, source_target_pairs={{252,0},{0,4},{4,8},{8,12},{12,16},{16,20},{20,24},{24,28},{28,32}... | collective-permute-start | bytes 98312 | tf_op jit(solution)/shard_map/ppermute | solution.py:12
  189.9 37.0 %collective-permute-start.13 = (f32[64,128]{1,0:T(8,128)}, f32[64,128]{1,0:T(8,128)S(1)}, u32[]{:S(2)}, u32[]{:S(2)}) collective-permute-start(f32[64,128]{1,0:T(8,128)} %get-tuple-element.54), channel_id=1, source_target_pairs={{4,0},{8,4},{12,8},{16,12},{20,16},{24,20},{28,24},{32,28},{36,32}... | collective-permute-start | bytes 98312 | tf_op jit(solution)/shard_map/ppermute | solution.py:12
  195.0 33.9 %collective-permute-start.14 = (f32[64,128]{1,0:T(8,128)}, f32[64,128]{1,0:T(8,128)}, u32[]{:S(2)}, u32[]{:S(2)}) collective-permute-start(f32[64,128]{1,0:T(8,128)} %get-tuple-element.53), channel_id=1, source_target_pairs={{248,0},{252,4},{0,8},{4,12},{8,16},{12,20},{16,24},{20,28},{24,32... | collective-permute-start | bytes 98312 | tf_op jit(solution)/shard_map/ppermute | solution.py:12
  196.5 39.0 %collective-permute-start.15 = (f32[64,128]{1,0:T(8,128)}, f32[64,128]{1,0:T(8,128)}, u32[]{:S(2)}, u32[]{:S(2)}) collective-permute-start(f32[64,128]{1,0:T(8,128)} %get-tuple-element.52), channel_id=1, source_target_pairs={{8,0},{12,4},{16,8},{20,12},{24,16},{28,20},{32,24},{36,28},{40,32... | collective-permute-start | bytes 98312 | tf_op jit(solution)/shard_map/ppermute | solution.py:12
  220.6 31.6 %collective-permute-start.44 = (f32[64,128]{0,1:T(8,128)}, f32[64,128]{0,1:T(8,128)}, u32[]{:S(2)}, u32[]{:S(2)}) collective-permute-start(f32[64,128]{0,1:T(8,128)} %get-tuple-element.23), channel_id=1, source_target_pairs={{252,0},{0,4},{4,8},{8,12},{12,16},{16,20},{20,24},{24,28},{28,32}... | collective-permute-start | bytes 98312 | tf_op jit(solution)/shard_map/ppermute | solution.py:12
  222.5 35.0 %collective-permute-start.45 = (f32[64,128]{0,1:T(8,128)}, f32[64,128]{0,1:T(8,128)S(1)}, u32[]{:S(2)}, u32[]{:S(2)}) collective-permute-start(f32[64,128]{0,1:T(8,128)} %get-tuple-element.22), channel_id=1, source_target_pairs={{4,0},{8,4},{12,8},{16,12},{20,16},{24,20},{28,24},{32,28},{36,32}... | collective-permute-start | bytes 98312 | tf_op jit(solution)/shard_map/ppermute | solution.py:12
  227.5 30.6 %collective-permute-start.46 = (f32[64,128]{0,1:T(8,128)}, f32[64,128]{0,1:T(8,128)S(1)}, u32[]{:S(2)}, u32[]{:S(2)}) collective-permute-start(f32[64,128]{0,1:T(8,128)} %get-tuple-element.21), channel_id=1, source_target_pairs={{248,0},{252,4},{0,8},{4,12},{8,16},{12,20},{16,24},{20,28},{24,32... | collective-permute-start | bytes 98312 | tf_op jit(solution)/shard_map/ppermute | solution.py:12
  228.9 34.8 %collective-permute-start.47 = (f32[64,128]{0,1:T(8,128)}, f32[64,128]{0,1:T(8,128)}, u32[]{:S(2)}, u32[]{:S(2)}) collective-permute-start(f32[64,128]{0,1:T(8,128)} %get-tuple-element.20), channel_id=1, source_target_pairs={{8,0},{12,4},{16,8},{20,12},{24,16},{28,20},{32,24},{36,28},{40,32... | collective-permute-start | bytes 98312 | tf_op jit(solution)/shard_map/ppermute | solution.py:12
  250.4 30.9 %collective-permute-start.16 = (f32[64,128]{1,0:T(8,128)}, f32[64,128]{1,0:T(8,128)}, u32[]{:S(2)}, u32[]{:S(2)}) collective-permute-start(f32[64,128]{1,0:T(8,128)} %get-tuple-element.51), channel_id=1, source_target_pairs={{252,0},{0,4},{4,8},{8,12},{12,16},{16,20},{20,24},{24,28},{28,32}... | collective-permute-start | bytes 98312 | tf_op jit(solution)/shard_map/ppermute | solution.py:12
  252.2 33.6 %collective-permute-start.17 = (f32[64,128]{1,0:T(8,128)}, f32[64,128]{1,0:T(8,128)}, u32[]{:S(2)}, u32[]{:S(2)}) collective-permute-start(f32[64,128]{1,0:T(8,128)} %get-tuple-element.50), channel_id=1, source_target_pairs={{4,0},{8,4},{12,8},{16,12},{20,16},{24,20},{28,24},{32,28},{36,32}... | collective-permute-start | bytes 98312 | tf_op jit(solution)/shard_map/ppermute | solution.py:12
  257.5 29.2 %collective-permute-start.18 = (f32[64,128]{1,0:T(8,128)}, f32[64,128]{1,0:T(8,128)}, u32[]{:S(2)}, u32[]{:S(2)}) collective-permute-start(f32[64,128]{1,0:T(8,128)} %get-tuple-element.49), channel_id=1, source_target_pairs={{248,0},{252,4},{0,8},{4,12},{8,16},{12,20},{16,24},{20,28},{24,32... | collective-permute-start | bytes 98312 | tf_op jit(solution)/shard_map/ppermute | solution.py:12
  258.1 34.3 %collective-permute-start.19 = (f32[64,128]{1,0:T(8,128)}, f32[64,128]{1,0:T(8,128)}, u32[]{:S(2)}, u32[]{:S(2)}) collective-permute-start(f32[64,128]{1,0:T(8,128)} %get-tuple-element.48), channel_id=1, source_target_pairs={{8,0},{12,4},{16,8},{20,12},{24,16},{28,20},{32,24},{36,28},{40,32... | collective-permute-start | bytes 98312 | tf_op jit(solution)/shard_map/ppermute | solution.py:12
  279.5 27.5 %collective-permute-start.48 = (f32[64,128]{0,1:T(8,128)}, f32[64,128]{0,1:T(8,128)}, u32[]{:S(2)}, u32[]{:S(2)}) collective-permute-start(f32[64,128]{0,1:T(8,128)} %get-tuple-element.19), channel_id=1, source_target_pairs={{252,0},{0,4},{4,8},{8,12},{12,16},{16,20},{20,24},{24,28},{28,32}... | collective-permute-start | bytes 98312 | tf_op jit(solution)/shard_map/ppermute | solution.py:12
  281.3 30.9 %collective-permute-start.49 = (f32[64,128]{0,1:T(8,128)}, f32[64,128]{0,1:T(8,128)S(1)}, u32[]{:S(2)}, u32[]{:S(2)}) collective-permute-start(f32[64,128]{0,1:T(8,128)} %get-tuple-element.18), channel_id=1, source_target_pairs={{4,0},{8,4},{12,8},{16,12},{20,16},{24,20},{28,24},{32,28},{36,32}... | collective-permute-start | bytes 98312 | tf_op jit(solution)/shard_map/ppermute | solution.py:12
  285.9 26.9 %collective-permute-start.50 = (f32[64,128]{0,1:T(8,128)}, f32[64,128]{0,1:T(8,128)S(1)}, u32[]{:S(2)}, u32[]{:S(2)}) collective-permute-start(f32[64,128]{0,1:T(8,128)} %get-tuple-element.17), channel_id=1, source_target_pairs={{248,0},{252,4},{0,8},{4,12},{8,16},{12,20},{16,24},{20,28},{24,32... | collective-permute-start | bytes 98312 | tf_op jit(solution)/shard_map/ppermute | solution.py:12
  286.6 31.8 %collective-permute-start.51 = (f32[64,128]{0,1:T(8,128)}, f32[64,128]{0,1:T(8,128)}, u32[]{:S(2)}, u32[]{:S(2)}) collective-permute-start(f32[64,128]{0,1:T(8,128)} %get-tuple-element.16), channel_id=1, source_target_pairs={{8,0},{12,4},{16,8},{20,12},{24,16},{28,20},{32,24},{36,28},{40,32... | collective-permute-start | bytes 98312 | tf_op jit(solution)/shard_map/ppermute | solution.py:12
  305.0 31.1 %collective-permute-start.20 = (f32[64,128]{1,0:T(8,128)S(1)}, f32[64,128]{1,0:T(8,128)S(1)}, u32[]{:S(2)}, u32[]{:S(2)}) collective-permute-start(f32[64,128]{1,0:T(8,128)S(1)} %get-tuple-element.47), channel_id=1, source_target_pairs={{252,0},{0,4},{4,8},{8,12},{12,16},{16,20},{20,24},{24,28},{28,32}... | collective-permute-start | bytes 98312 | tf_op jit(solution)/shard_map/ppermute | solution.py:12
  306.9 33.0 %collective-permute-start.21 = (f32[64,128]{1,0:T(8,128)S(1)}, f32[64,128]{1,0:T(8,128)S(1)}, u32[]{:S(2)}, u32[]{:S(2)}) collective-permute-start(f32[64,128]{1,0:T(8,128)S(1)} %get-tuple-element.46), channel_id=1, source_target_pairs={{4,0},{8,4},{12,8},{16,12},{20,16},{24,20},{28,24},{32,28},{36,32}... | collective-permute-start | bytes 98312 | tf_op jit(solution)/shard_map/ppermute | solution.py:12
  312.2 27.8 %collective-permute-start.22 = (f32[64,128]{1,0:T(8,128)S(1)}, f32[64,128]{1,0:T(8,128)S(1)}, u32[]{:S(2)}, u32[]{:S(2)}) collective-permute-start(f32[64,128]{1,0:T(8,128)S(1)} %get-tuple-element.45), channel_id=1, source_target_pairs={{248,0},{252,4},{0,8},{4,12},{8,16},{12,20},{16,24},{20,28},{24,32... | collective-permute-start | bytes 98312 | tf_op jit(solution)/shard_map/ppermute | solution.py:12
  312.8 32.4 %collective-permute-start.23 = (f32[64,128]{1,0:T(8,128)S(1)}, f32[64,128]{1,0:T(8,128)S(1)}, u32[]{:S(2)}, u32[]{:S(2)}) collective-permute-start(f32[64,128]{1,0:T(8,128)S(1)} %get-tuple-element.44), channel_id=1, source_target_pairs={{8,0},{12,4},{16,8},{20,12},{24,16},{28,20},{32,24},{36,28},{40,32... | collective-permute-start | bytes 98312 | tf_op jit(solution)/shard_map/ppermute | solution.py:12
  334.3 25.5 %collective-permute-start.52 = (f32[64,128]{0,1:T(8,128)}, f32[64,128]{0,1:T(8,128)}, u32[]{:S(2)}, u32[]{:S(2)}) collective-permute-start(f32[64,128]{0,1:T(8,128)} %get-tuple-element.15), channel_id=1, source_target_pairs={{252,0},{0,4},{4,8},{8,12},{12,16},{16,20},{20,24},{24,28},{28,32}... | collective-permute-start | bytes 98312 | tf_op jit(solution)/shard_map/ppermute | solution.py:12
  336.1 28.8 %collective-permute-start.53 = (f32[64,128]{0,1:T(8,128)}, f32[64,128]{0,1:T(8,128)S(1)}, u32[]{:S(2)}, u32[]{:S(2)}) collective-permute-start(f32[64,128]{0,1:T(8,128)} %get-tuple-element.14), channel_id=1, source_target_pairs={{4,0},{8,4},{12,8},{16,12},{20,16},{24,20},{28,24},{32,28},{36,32}... | collective-permute-start | bytes 98312 | tf_op jit(solution)/shard_map/ppermute | solution.py:12
  339.9 25.6 %collective-permute-start.54 = (f32[64,128]{0,1:T(8,128)}, f32[64,128]{0,1:T(8,128)S(1)}, u32[]{:S(2)}, u32[]{:S(2)}) collective-permute-start(f32[64,128]{0,1:T(8,128)} %get-tuple-element.13), channel_id=1, source_target_pairs={{248,0},{252,4},{0,8},{4,12},{8,16},{12,20},{16,24},{20,28},{24,32... | collective-permute-start | bytes 98312 | tf_op jit(solution)/shard_map/ppermute | solution.py:12
  340.0 31.0 %collective-permute-start.55 = (f32[64,128]{0,1:T(8,128)}, f32[64,128]{0,1:T(8,128)}, u32[]{:S(2)}, u32[]{:S(2)}) collective-permute-start(f32[64,128]{0,1:T(8,128)} %get-tuple-element.12), channel_id=1, source_target_pairs={{8,0},{12,4},{16,8},{20,12},{24,16},{28,20},{32,24},{36,28},{40,32... | collective-permute-start | bytes 98312 | tf_op jit(solution)/shard_map/ppermute | solution.py:12
  357.8 30.9 %collective-permute-start.24 = (f32[64,128]{1,0:T(8,128)}, f32[64,128]{1,0:T(8,128)}, u32[]{:S(2)}, u32[]{:S(2)}) collective-permute-start(f32[64,128]{1,0:T(8,128)} %get-tuple-element.43), channel_id=1, source_target_pairs={{252,0},{0,4},{4,8},{8,12},{12,16},{16,20},{20,24},{24,28},{28,32}... | collective-permute-start | bytes 98312 | tf_op jit(solution)/shard_map/ppermute | solution.py:12
  359.7 33.5 %collective-permute-start.25 = (f32[64,128]{1,0:T(8,128)}, f32[64,128]{1,0:T(8,128)}, u32[]{:S(2)}, u32[]{:S(2)}) collective-permute-start(f32[64,128]{1,0:T(8,128)} %get-tuple-element.42), channel_id=1, source_target_pairs={{4,0},{8,4},{12,8},{16,12},{20,16},{24,20},{28,24},{32,28},{36,32}... | collective-permute-start | bytes 98312 | tf_op jit(solution)/shard_map/ppermute | solution.py:12
  364.9 29.1 %collective-permute-start.26 = (f32[64,128]{1,0:T(8,128)}, f32[64,128]{1,0:T(8,128)}, u32[]{:S(2)}, u32[]{:S(2)}) collective-permute-start(f32[64,128]{1,0:T(8,128)} %get-tuple-element.41), channel_id=1, source_target_pairs={{248,0},{252,4},{0,8},{4,12},{8,16},{12,20},{16,24},{20,28},{24,32... | collective-permute-start | bytes 98312 | tf_op jit(solution)/shard_map/ppermute | solution.py:12
  365.5 34.3 %collective-permute-start.27 = (f32[64,128]{1,0:T(8,128)}, f32[64,128]{1,0:T(8,128)}, u32[]{:S(2)}, u32[]{:S(2)}) collective-permute-start(f32[64,128]{1,0:T(8,128)} %get-tuple-element.40), channel_id=1, source_target_pairs={{8,0},{12,4},{16,8},{20,12},{24,16},{28,20},{32,24},{36,28},{40,32... | collective-permute-start | bytes 98312 | tf_op jit(solution)/shard_map/ppermute | solution.py:12
  386.8 28.1 %collective-permute-start.56 = (f32[64,128]{0,1:T(8,128)}, f32[64,128]{0,1:T(8,128)}, u32[]{:S(2)}, u32[]{:S(2)}) collective-permute-start(f32[64,128]{0,1:T(8,128)} %get-tuple-element.11), channel_id=1, source_target_pairs={{252,0},{0,4},{4,8},{8,12},{12,16},{16,20},{20,24},{24,28},{28,32}... | collective-permute-start | bytes 98312 | tf_op jit(solution)/shard_map/ppermute | solution.py:12
  388.7 31.4 %collective-permute-start.57 = (f32[64,128]{0,1:T(8,128)}, f32[64,128]{0,1:T(8,128)S(1)}, u32[]{:S(2)}, u32[]{:S(2)}) collective-permute-start(f32[64,128]{0,1:T(8,128)} %get-tuple-element.10), channel_id=1, source_target_pairs={{4,0},{8,4},{12,8},{16,12},{20,16},{24,20},{28,24},{32,28},{36,32}... | collective-permute-start | bytes 98312 | tf_op jit(solution)/shard_map/ppermute | solution.py:12
  393.2 27.5 %collective-permute-start.58 = (f32[64,128]{0,1:T(8,128)}, f32[64,128]{0,1:T(8,128)S(1)}, u32[]{:S(2)}, u32[]{:S(2)}) collective-permute-start(f32[64,128]{0,1:T(8,128)} %get-tuple-element.9), channel_id=1, source_target_pairs={{248,0},{252,4},{0,8},{4,12},{8,16},{12,20},{16,24},{20,28},{24,32... | collective-permute-start | bytes 98312 | tf_op jit(solution)/shard_map/ppermute | solution.py:12
  394.0 32.4 %collective-permute-start.59 = (f32[64,128]{0,1:T(8,128)}, f32[64,128]{0,1:T(8,128)}, u32[]{:S(2)}, u32[]{:S(2)}) collective-permute-start(f32[64,128]{0,1:T(8,128)} %get-tuple-element.8), channel_id=1, source_target_pairs={{8,0},{12,4},{16,8},{20,12},{24,16},{28,20},{32,24},{36,28},{40,32... | collective-permute-start | bytes 98312 | tf_op jit(solution)/shard_map/ppermute | solution.py:12
  413.0 30.4 %collective-permute-start.28 = (f32[64,128]{1,0:T(8,128)}, f32[64,128]{1,0:T(8,128)}, u32[]{:S(2)}, u32[]{:S(2)}) collective-permute-start(f32[64,128]{1,0:T(8,128)} %get-tuple-element.39), channel_id=1, source_target_pairs={{252,0},{0,4},{4,8},{8,12},{12,16},{16,20},{20,24},{24,28},{28,32}... | collective-permute-start | bytes 98312 | tf_op jit(solution)/shard_map/ppermute | solution.py:12
  414.9 33.1 %collective-permute-start.29 = (f32[64,128]{1,0:T(8,128)}, f32[64,128]{1,0:T(8,128)}, u32[]{:S(2)}, u32[]{:S(2)}) collective-permute-start(f32[64,128]{1,0:T(8,128)} %get-tuple-element.38), channel_id=1, source_target_pairs={{4,0},{8,4},{12,8},{16,12},{20,16},{24,20},{28,24},{32,28},{36,32}... | collective-permute-start | bytes 98312 | tf_op jit(solution)/shard_map/ppermute | solution.py:12
  420.1 28.7 %collective-permute-start.30 = (f32[64,128]{1,0:T(8,128)}, f32[64,128]{1,0:T(8,128)}, u32[]{:S(2)}, u32[]{:S(2)}) collective-permute-start(f32[64,128]{1,0:T(8,128)} %get-tuple-element.37), channel_id=1, source_target_pairs={{248,0},{252,4},{0,8},{4,12},{8,16},{12,20},{16,24},{20,28},{24,32... | collective-permute-start | bytes 98312 | tf_op jit(solution)/shard_map/ppermute | solution.py:12
  420.7 33.9 %collective-permute-start.31 = (f32[64,128]{1,0:T(8,128)}, f32[64,128]{1,0:T(8,128)}, u32[]{:S(2)}, u32[]{:S(2)}) collective-permute-start(f32[64,128]{1,0:T(8,128)} %get-tuple-element.36), channel_id=1, source_target_pairs={{8,0},{12,4},{16,8},{20,12},{24,16},{28,20},{32,24},{36,28},{40,32... | collective-permute-start | bytes 98312 | tf_op jit(solution)/shard_map/ppermute | solution.py:12
  441.5 13.9 %collective-permute-start.60 = (f32[64,128]{0,1:T(8,128)S(1)}, f32[64,128]{0,1:T(8,128)S(1)}, u32[]{:S(2)}, u32[]{:S(2)}) collective-permute-start(f32[64,128]{0,1:T(8,128)S(1)} %get-tuple-element.7), channel_id=1, source_target_pairs={{252,0},{0,4},{4,8},{8,12},{12,16},{16,20},{20,24},{24,28},{28,32}... | collective-permute-start | bytes 98312 | tf_op jit(solution)/shard_map/ppermute | solution.py:12
  443.4 12.6 %collective-permute-start.61 = (f32[64,128]{0,1:T(8,128)S(1)}, f32[64,128]{0,1:T(8,128)S(1)}, u32[]{:S(2)}, u32[]{:S(2)}) collective-permute-start(f32[64,128]{0,1:T(8,128)S(1)} %get-tuple-element.6), channel_id=1, source_target_pairs={{4,0},{8,4},{12,8},{16,12},{20,16},{24,20},{28,24},{32,28},{36,32}... | collective-permute-start | bytes 98312 | tf_op jit(solution)/shard_map/ppermute | solution.py:12
  448.0 8.6 %collective-permute-start.62 = (f32[64,128]{0,1:T(8,128)S(1)}, f32[64,128]{0,1:T(8,128)S(1)}, u32[]{:S(2)}, u32[]{:S(2)}) collective-permute-start(f32[64,128]{0,1:T(8,128)S(1)} %get-tuple-element.5), channel_id=1, source_target_pairs={{248,0},{252,4},{0,8},{4,12},{8,16},{12,20},{16,24},{20,28},{24,32... | collective-permute-start | bytes 98312 | tf_op jit(solution)/shard_map/ppermute | solution.py:12
  448.8 10.5 %collective-permute-start.63 = (f32[64,128]{0,1:T(8,128)S(1)}, f32[64,128]{0,1:T(8,128)S(1)}, u32[]{:S(2)}, u32[]{:S(2)}) collective-permute-start(f32[64,128]{0,1:T(8,128)S(1)} %get-tuple-element.4), channel_id=1, source_target_pairs={{8,0},{12,4},{16,8},{20,12},{24,16},{28,20},{32,24},{36,28},{40,32... | collective-permute-start | bytes 98312 | tf_op jit(solution)/shard_map/ppermute | solution.py:12
  (17 other events, 159.5 us)
Sparse Core Ops, SparseCore 0:
  471.8 182.5 all-reduce.1
where the time goes:
time: 673 us; the launch traced here: 664 us
  waiting for transfers between devices  189 us (28%)
  starting transfers between devices  164 us (24%)
  matrix products  131 us (19%)
  local copies, waits for them, and re-layouts  127 us (19%)
  blocking collectives  22.7 us (3%)
  between operations  15.6 us (2%)
  other arithmetic  13 us (2%)
    psum x1, waiting for transfers between devices, local(): summed = lax.psum(local_grads, 'dom')  174 us
    ppermute x64, starting transfers between devices, from_behind(): return lax.ppermute(block, axis, route)  164 us
    dot_general x16, matrix products, apply_operator(): jnp.einsum('ctj,tjk->ctk', picked, tile_values, precision=lax.Precision.H...  107 us
    unnamed x82, local copies, waits for them, and re-layouts  37.6 us
    gather x16, local copies, waits for them, and re-layouts, apply_operator(): picked = jnp.take(blocks, tile_cols.reshape(-1), axis=1)  31.3 us
    gather x24, local copies, waits for them, and re-layouts, apply_operator(): outgoing = jnp.take(field_in, send_list[0], axis=1)  18.1 us
    ppermute x64, waiting for transfers between devices, from_behind(): return lax.ppermute(block, axis, route)  14.7 us
    concatenate x16, local copies, waits for them, and re-layouts, apply_operator(): extended = jnp.concatenate([field_in] + received, axis=1)  14.5 us
  transfers between devices with their start and end apart: 65, of which 4 were waited for; matrix products, arithmetic and copies ran while one was open for 36% of the time, Pallas kernels for 0%

commit v1 on v0

v1 whole, which is shorter than its diff:
```python
import functools

import jax
import jax.numpy as jnp
from jax import lax
from jax.experimental import pallas as pl
from jax.experimental.pallas import tpu as pltpu
from jax.sharding import PartitionSpec as P

NEIGHBOUR_SHIFTS = (1, -1, 2, -2)
SLOTS = len(NEIGHBOUR_SHIFTS)
MESH = pl.DeviceIdType.MESH
F32, BF16 = jnp.float32, jnp.bfloat16


def dot(a, b):
    return jnp.dot(a, b, preferred_element_type=F32)


def dot_nt(a, b):
    return lax.dot_general(a, b, (((1,), (1,)), ((), ())), preferred_element_type=F32)


def split(x):
    hi = x.astype(BF16)
    return hi, (x - hi.astype(F32)).astype(BF16)


def kernel(
    dims,
    feat_hbm, cot_hbm, w_hbm, tiles_hbm, cols_hbm, send_hbm,
    grad_out, wg_out,
    feat, cotx, w, tiles, cols, send, sel, e_hi, e_lo, state, parts, base,
    outbox, inbox, wg, wg_rows, wg_deep, wg_full,
    local_sem, tile_sem, out_sem, gather_send, gather_recv, halo_send, halo_recv,
    s1, s2, s3, r1, r2, r3,
):
    dom, chan, group, scale = dims
    depth = dom // group
    me, xc = lax.axis_index("dom"), lax.axis_index("chan")
    zc, bc = me // group, lax.rem(me, group)
    top = w.shape[0] - 1
    c, n = feat_hbm.shape
    tile = tiles.shape[-1]
    halo = SLOTS * tile
    blocks = n // tile
    wide = n + halo
    per_row = tiles.shape[0] // blocks
    share = c // group

    def along_dom(index):
        return {"dom": index}

    halo_to = [along_dom(lax.rem(me + d + dom, dom)) for d in NEIGHBOUR_SHIFTS]
    chan_of = [lax.rem(xc + j, chan) for j in range(1, chan)]
    row_of = [lax.rem(bc + j, group) for j in range(1, group)]
    deep_of = [lax.rem(zc + j, depth) for j in range(1, depth)]
    row_to = [along_dom(zc * group + b) for b in row_of]
    deep_to = [along_dom(z * group + bc) for z in deep_of]

    def remote(src, dst, ssem, rsem, to):
        return pltpu.make_async_remote_copy(src, dst, ssem, rsem, device_id=to, device_id_type=MESH)

    my_rows = pl.ds(pl.multiple_of(xc * c, c), c)
    own_cot = cotx.at[my_rows, pl.ds(0, n)]
    own_feat = feat.at[my_rows, :]
    in_copies = [
        pltpu.make_async_copy(send_hbm, send, local_sem.at[0]),
        pltpu.make_async_copy(cot_hbm, own_cot, local_sem.at[1]),
        pltpu.make_async_copy(cols_hbm, cols, local_sem.at[2]),
        pltpu.make_async_copy(w_hbm, w, local_sem.at[3]),
        pltpu.make_async_copy(feat_hbm, own_feat, local_sem.at[4]),
    ]
    for copy in in_copies:
        copy.start()

    def tile_copy(r):
        rows = pl.ds(r * per_row, per_row)
        return pltpu.make_async_copy(tiles_hbm.at[rows], tiles.at[rows], tile_sem.at[r])

    for r in range(blocks):
        tile_copy(r).start()

    barrier = pltpu.get_barrier_semaphore()
    greeted = halo_to + [{"chan": x} for x in chan_of] + row_to + deep_to
    for peer in greeted:
        pl.semaphore_signal(barrier, inc=1, device_id=peer, device_id_type=MESH)

    in_copies[0].wait()
    node = lax.broadcasted_iota(jnp.int32, (n, tile), 0)
    for s in range(SLOTS):
        picked = send[0, s : s + 1, :]
        sel[:, s * tile : (s + 1) * tile] = jnp.where(node == picked, 1.0, 0.0).astype(BF16)
    in_copies[1].wait()
    first = cotx[my_rows, 0:n]
    first_sel = dot(first, sel[...])
    state[0, 0:c, 0:n] = first.astype(F32)
    state[0, 0:c, n:wide] = first_sel
    state[0, c:, :] = jnp.zeros((c, wide), F32)
    state[1] = jnp.zeros((2 * c, wide), F32)
    parts[...] = jnp.zeros(parts.shape, BF16)
    parts[0:c] = first
    for s in range(SLOTS):
        outbox[0, s] = jnp.zeros(outbox.shape[2:], BF16)
        outbox[0, s, 0:c] = first_sel[:, s * tile : (s + 1) * tile].astype(BF16)

    def halo_copy(parity, s):
        return remote(
            outbox.at[parity, s], inbox.at[parity, s], halo_send.at[parity, s], halo_recv.at[parity, s], halo_to[s]
        )

    def gather_copy(which, j):
        src = (cot_hbm, feat_hbm)[which]
        dst = (own_cot, own_feat)[which]
        return remote(src, dst, gather_send.at[which, j], gather_recv.at[which, xc], {"chan": chan_of[j]})

    def gather_wait(which):
        for x in chan_of:
            rows = pl.ds(pl.multiple_of(x * c, c), c)
            dst = (cotx.at[rows, pl.ds(0, n)], feat.at[rows, :])[which]
            src = (cot_hbm, feat_hbm)[which]
            remote(src, dst, gather_send.at[which, 0], gather_recv.at[which, x], {"chan": x}).wait_recv()

    pl.semaphore_wait(barrier, len(greeted))
    for s in range(SLOTS):
        halo_copy(0, s).start()
    for which in range(2):
        for j in range(chan - 1):
            gather_copy(which, j).start()

    in_copies[2].wait()

    def assemble(r, carry):
        tile_copy(r).wait()
        columns = pl.ds(pl.multiple_of(r * tile, tile), tile)
        marks = [cols[0, r, j] for j in range(per_row)]

        def block(cb, carry):
            total = jnp.zeros((tile, tile), F32)
            for j in range(per_row):
                total += jnp.where(marks[j] == cb, 1.0, 0.0) * tiles[r * per_row + j]
            hi, lo = split(total)
            rows = pl.ds(pl.multiple_of(cb * tile, tile), tile)
            e_hi[rows, columns] = hi
            e_lo[rows, columns] = lo
            return carry

        return lax.fori_loop(0, blocks + SLOTS, block, carry)

    lax.fori_loop(0, blocks, assemble, 0)

    def extend(i, carry):
        rows = pl.ds(pl.multiple_of(i * 2 * tile, 2 * tile), 2 * tile)
        e_hi[rows, n:wide] = dot(e_hi[rows, 0:n], sel[...]).astype(BF16)
        e_lo[rows, n:wide] = dot(e_lo[rows, 0:n], sel[...]).astype(BF16)
        return carry

    lax.fori_loop(0, wide // (2 * tile), extend, 0)

    in_copies[3].wait()
    gather_wait(0)
    cotx[:, n:wide] = dot(cotx[:, 0:n], sel[...]).astype(BF16)

    chunk = halo

    def prepare(order, fac_u, fac_b, older):
        for i in range(wide // chunk):
            at = slice(i * chunk, (i + 1) * chunk)
            full = dot(parts[...], e_hi[0:n, at])
            part = full[0 : 2 * c] + full[2 * c :] + dot(parts[0 : 2 * c], e_lo[0:n, at])
            base[0:c, at] = fac_u * part[0:c] - state[older, 0:c, at]
            base[c:, at] = fac_b * part[c:] + dot(w[order], cotx[:, at]) - state[older, c:, at]

    def arrived(lhs, at):
        full = dot(lhs, e_hi[n:wide, at])
        return full[0 : 2 * c] + full[2 * c :] + dot(lhs[0 : 2 * c], e_lo[n:wide, at])

    def halo_in(parity):
        for s in range(SLOTS):
            halo_copy(parity, s).wait_recv()
        return jnp.concatenate([inbox[parity, s] for s in range(SLOTS)], axis=1)

    def row_part(b):
        return pl.ds(pl.multiple_of(b * share, share), share)

    def step1(k, j, sem_of):
        return remote(wg.at[k, row_part(row_of[j])], wg_rows.at[k, sem_of], s1.at[j], r1.at[k, sem_of], row_to[j])

    def step2(k, j, sem_of):
        return remote(wg_deep.at[k, sem_of], wg_deep.at[k, sem_of], s2.at[j], r2.at[k, sem_of], deep_to[j])

    def step3(k, j, sem_of):
        part = wg_full.at[k, row_part(sem_of)]
        return remote(part, part, s3.at[j], r3.at[k, sem_of], row_to[j])

    def send_rows(k, again):
        for j in range(group - 1):
            if again:
                step1(k, j, bc).wait_send()
        wg_rows[k, bc] = wg[k, row_part(bc), :]
        for j in range(group - 1):
            step1(k, j, bc).start()

    def send_deep(k, again):
        for j in range(group - 1):
            step1(k, j, row_of[j]).wait_recv()
        for j in range(depth - 1):
            if again:
                step2(k, j, zc).wait_send()
        total = wg_rows[k, 0]
        for j in range(1, group):
            total += wg_rows[k, j]
        wg_deep[k, zc] = total
        for j in range(depth - 1):
            step2(k, j, zc).start()

    def send_back(k, again):
        for j in range(depth - 1):
            step2(k, j, deep_of[j]).wait_recv()
        for j in range(group - 1):
            if again:
                step3(k, j, bc).wait_send()
        total = wg_deep[k, 0]
        for j in range(1, depth):
            total += wg_deep[k, j]
        wg_full[k, row_part(bc), :] = total * scale
        for j in range(group - 1):
            step3(k, j, bc).start()

    prepare(top, 1.0, 2.0, 1)

    def round_(r, carry):
        parity = lax.rem(r, 2)
        other = 1 - parity
        fac_u = jnp.where(r == 0, 1.0, 2.0).astype(F32)
        lhs = halo_in(parity)
        at = slice(n, wide)
        got = arrived(lhs, at)
        next_u = base[0:c, at] + fac_u * got[0:c]
        next_b = base[c:, at] + 2.0 * got[c:]
        state[other, 0:c, at] = next_u
        state[other, c:, at] = next_b
        u_hi, u_lo = split(next_u)
        b_hi, b_lo = split(next_b)

        @pl.when(r > 0)
        def _():
            for s in range(SLOTS):
                halo_copy(other, s).wait_send()

        for s in range(SLOTS):
            cut = slice(s * tile, (s + 1) * tile)
            for i, piece in enumerate((u_hi, b_hi, u_lo, b_lo)):
                outbox[other, s, i * c : (i + 1) * c] = piece[:, cut]
        for s in range(SLOTS):
            halo_copy(other, s).start()
        for i in range(n // chunk):
            at = slice(i * chunk, (i + 1) * chunk)
            got = arrived(lhs, at)
            next_u = base[0:c, at] + fac_u * got[0:c]
            next_b = base[c:, at] + 2.0 * got[c:]
            state[other, 0:c, at] = next_u
            state[other, c:, at] = next_b
            for j, piece in enumerate((*split(next_u), *split(next_b))):
                row = (0, 2, 1, 3)[j] * c
                parts[row : row + c, at] = piece

        @pl.when(r == 0)
        def _():
            in_copies[4].wait()
            gather_wait(1)
            wg[0] = dot_nt(cotx[my_rows, 0:n], feat[...])
            send_rows(0, False)

        both = dot_nt(jnp.concatenate([parts[0:c], parts[2 * c : 3 * c]], axis=0), feat[...])
        wg[r + 1] = both[0:c] + both[c:]
        prepare(top - 1 - r, 2.0, jnp.where(r == top - 1, 1.0, 2.0).astype(F32), parity)

        @pl.when(r == 2)
        def _():
            send_back(0, False)

        @pl.when(r >= 2)
        def _():
            send_back(r - 1, True)

        @pl.when(r == 1)
        def _():
            send_deep(0, False)

        @pl.when(r >= 1)
        def _():
            send_deep(r, True)

        send_rows(r + 1, True)
        return carry

    lax.fori_loop(0, top, round_, 0)

    send_deep(top, True)
    last = top % 2
    lhs = halo_in(last)
    for i in range(n // chunk):
        at = slice(i * chunk, (i + 1) * chunk)
        base[c:, at] = base[c:, at] + arrived(lhs, at)[c:]
    grad_copy = pltpu.make_async_copy(base.at[pl.ds(c, c), pl.ds(0, n)], grad_out, out_sem.at[0])
    grad_copy.start()
    send_back(top - 1, True)
    for k in range(top):
        for j in range(group - 1):
            step3(k, j, row_of[j]).wait_recv()
    early = pltpu.make_async_copy(wg_full.at[pl.ds(0, top)], wg_out.at[pl.ds(0, top)], out_sem.at[1])
    early.start()
    send_back(top, True)
    for j in range(group - 1):
        step3(top, j, row_of[j]).wait_recv()
    late = pltpu.make_async_copy(wg_full.at[top], wg_out.at[top], out_sem.at[2])
    late.start()

    for which in range(2):
        for j in range(chan - 1):
            gather_copy(which, j).wait_send()
    for parity in range(2):
        for s in range(SLOTS):
            halo_copy(parity, s).wait_send()
    for j in range(group - 1):
        step1(top, j, bc).wait_send()
        step3(top, j, bc).wait_send()
    for j in range(depth - 1):
        step2(top, j, zc).wait_send()
    grad_copy.wait()
    early.wait()
    late.wait()


def local(dom, chan, group, features, cotangent, weights, tile_values, tile_cols, send_list):
    c, n = features.shape
    orders, _, all_c = weights.shape
    tiles, tile, _ = tile_values.shape
    halo = SLOTS * tile
    wide = n + halo
    depth, share = dom // group, c // group
    scale = float(dom * n) ** -0.5
    dma, vmem = pltpu.SemaphoreType.DMA, pltpu.VMEM
    anywhere = pl.BlockSpec(memory_space=pl.ANY)
    input_grad, weight_grad = pl.pallas_call(
        functools.partial(kernel, (dom, chan, group, scale)),
        out_shape=(
            jax.ShapeDtypeStruct((c, n), F32),
            jax.ShapeDtypeStruct((orders, c, all_c), F32),
        ),
        in_specs=[anywhere] * 6,
        out_specs=(anywhere, anywhere),
        scratch_shapes=[
            vmem((all_c, n), BF16),
            vmem((all_c, wide), BF16),
            vmem(weights.shape, BF16),
            vmem(tile_values.shape, F32),
            pltpu.SMEM(tile_cols.shape, jnp.int32),
            vmem(send_list.shape, jnp.int32),
            vmem((n, halo), BF16),
            vmem((wide, wide), BF16),
            vmem((wide, wide), BF16),
            vmem((2, 2 * c, wide), F32),
            vmem((4 * c, n), BF16),
            vmem((2 * c, wide), F32),
            vmem((2, SLOTS, 4 * c, tile), BF16),
            vmem((2, SLOTS, 4 * c, tile), BF16),
            vmem((orders, c, all_c), F32),
            vmem((orders, group, share, all_c), F32),
            vmem((orders, depth, share, all_c), F32),
            vmem((orders, c, all_c), F32),
            dma((5,)),
            dma((n // tile,)),
            dma((3,)),
            dma((2, chan)),
            dma((2, chan)),
            dma((2, SLOTS)),
            dma((2, SLOTS)),
            dma((group,)),
            dma((depth,)),
            dma((group,)),
            dma((orders, group)),
            dma((orders, depth)),
            dma((orders, group)),
        ],
        compiler_params=pltpu.CompilerParams(
            collective_id=0, has_side_effects=True, vmem_limit_bytes=48 << 20
        ),
        name="clenshaw",
    )(features, cotangent, weights, tile_values, tile_cols, send_list)
    return input_grad, jnp.swapaxes(weight_grad, 1, 2)


def solution(mesh):
    dom, chan = mesh.shape["dom"], mesh.shape["chan"]
    placed = (
        P("chan", "dom"),
        P("chan", "dom"),
        P(None, "chan", None),
        P("dom", None, None),
        P("dom", None, None),
        P("dom", None, None),
    )
    return jax.shard_map(
        functools.partial(local, dom, chan, 8),
        mesh=mesh,
        in_specs=placed,
        out_specs=(P("chan", "dom"), P(None, None, "chan")),
        check_vma=False,
    )
```

time: 673 us -> 92.7 us (0.14); the launches traced: 664 us -> 92.4 us
  waiting for transfers between devices: 189 us -> 0 us
  starting transfers between devices: 164 us -> 0 us
  matrix products: 131 us -> 0 us
  local copies, waits for them, and re-layouts: 127 us -> 7.84 us
  Pallas kernels: 0 us -> 83.9 us
  blocking collectives: 22.7 us -> 0 us
  between operations: 15.6 us -> 0.65 us
  other arithmetic: 13 us -> 0 us
    psum x1 -> x0, waiting for transfers between devices: 174 us -> none  [local(): summed = lax.psum(local_grads, 'dom')]
    ppermute x64 -> x0, starting transfers between devices: 164 us -> none  [from_behind(): return lax.ppermute(block, axis, route)]
    dot_general x34 -> x0, matrix products: 131 us -> none  [the longest x16 107 us: apply_operator(): jnp.einsum('ctj,tjk->ctk', picked, tile_values, precision=lax.Precision.H...]
    pallas_call x0 -> x1, Pallas kernels: none -> 83.9 us  [local(): pl.pallas_call(functools.partial(kernel, (dom, chan, group, scale)), out_...]
    gather x40 -> x0, local copies, waits for them, and re-layouts: 49.3 us -> none  [the longest x16 31.3 us: apply_operator(): picked = jnp.take(blocks, tile_cols.reshape(-1), axis=1)]
    unnamed x82 -> x14, local copies, waits for them, and re-layouts: 37.6 us -> 7.84 us
    all_gather x2 -> x0, blocking collectives: 22.7 us -> none  [the longest x1 12.5 us: local(): lax.all_gather(cotangent, 'chan', axis=0, tiled=True)]
    ppermute x64 -> x0, waiting for transfers between devices: 14.7 us -> none  [from_behind(): return lax.ppermute(block, axis, route)]
  transfers between devices with their start and end apart: 65 -> 0, of which waited for: 4 -> 0; matrix products, arithmetic and copies ran while one was open for 36% -> 0% of each run, Pallas kernels for 0% -> 0%
where the time goes in v1:
time: 92.7 us; the launch traced here: 92.4 us
  Pallas kernels  83.9 us (91%)
  local copies, waits for them, and re-layouts  7.84 us (8%)
    pallas_call x1, Pallas kernels, local(): pl.pallas_call(functools.partial(kernel, (dom, chan, group, scale)), out_...  83.9 us
    unnamed x14, local copies, waits for them, and re-layouts  7.84 us

profile of v1, /device:TPU:1, one launch (start us, length us, event | category | flops | bytes accessed | tf_op | source)
XLA Modules:
  0.0 92.4 jit_solution(3376749843454482002)
XLA Ops:
  0.6 0.0 copy-start
  0.6 2.2 %copy-done = f32[64,128,128]{2,1,0:T(8,128)S(1)} copy-done((f32[64,128,128]{2,1,0:T(8,128)S(1)}, f32[64,128,128]{2,1,0:T(8,128)}, u32[]{:S(2)}) %copy-start) | copy-done | bytes 4194328
  2.8 0.0 copy-start.1
  2.8 1.0 %copy-done.1 = bf16[9,64,256]{2,1,0:T(8,128)(2,1)S(1)} copy-done((bf16[9,64,256]{2,1,0:T(8,128)(2,1)S(1)}, bf16[9,64,256]{2,1,0:T(8,128)(2,1)}, u32[]{:S(2)}) %copy-start.1) | copy-done | bytes 294936
  3.8 0.0 copy-start.2
  3.8 0.9 copy-done.2
  4.7 0.0 copy-start.3
  4.7 0.9 copy-done.3
  5.6 0.0 copy-start.4
  5.6 0.7 copy-done.4
  6.3 0.0 copy-start.5
  6.3 0.7 copy-done.5
  7.0 83.9 %clenshaw.1 = (f32[64,1024]{1,0:T(8,128)S(1)}, f32[9,64,256]{2,1,0:T(8,128)S(1)}) custom-call(bf16[64,1024]{1,0:T(8,128)(2,1)S(1)} %copy-done.2, bf16[64,1024]{1,0:T(8,128)(2,1)S(1)} %copy-done.3, bf16[9,64,256]{2,1,0:T(8,128)(2,1)S(1)} %copy-done.1, f32[64,128,128]{2,1,0:T(8,128)S(1)} %copy-done, s32[1,8,8]{2,1,0:T(8,128)S(1)} %copy-done.4, ...), custom_call_target="tpu_custom_call" | custom-call | tf_op jit(solution)/shard_map/clenshaw/pallas_call | solution.py:346
  90.9 0.7 copy.10
  91.6 0.8 copy.11
Async XLA Ops:
  0.6 2.2 %copy-start = (f32[64,128,128]{2,1,0:T(8,128)S(1)}, f32[64,128,128]{2,1,0:T(8,128)}, u32[]{:S(2)}) copy-start(f32[64,128,128]{2,1,0:T(8,128)} %tiles_hbm.1) | copy-start | bytes 12582916
  2.8 1.0 %copy-start.1 = (bf16[9,64,256]{2,1,0:T(8,128)(2,1)S(1)}, bf16[9,64,256]{2,1,0:T(8,128)(2,1)}, u32[]{:S(2)}) copy-start(bf16[9,64,256]{2,1,0:T(8,128)(2,1)} %w_hbm.1) | copy-start | bytes 884740
  3.8 0.9 copy-start.2
  4.7 0.9 copy-start.3
  5.6 0.7 copy-start.4
  6.3 0.7 copy-start.5

commit v2 on v1

--- a/solution.py
+++ b/solution.py
@@ -10,6 +10,7 @@
 NEIGHBOUR_SHIFTS = (1, -1, 2, -2)
 SLOTS = len(NEIGHBOUR_SHIFTS)
 MESH = pl.DeviceIdType.MESH
+BATCHES = ((0, 3), (3, 6), (6, 7), (7, 8), (8, 9))
 F32, BF16 = jnp.float32, jnp.bfloat16
 
 
@@ -30,8 +31,8 @@
     dims,
     feat_hbm, cot_hbm, w_hbm, tiles_hbm, cols_hbm, send_hbm,
     grad_out, wg_out,
-    feat, cotx, w, tiles, cols, send, sel, e_hi, e_lo, state, parts, base,
-    outbox, inbox, wg, wg_rows, wg_deep, wg_full,
+    feat, cotx, w, tiles, sums, cols, send, sel, e_hi, e_lo, state, parts, base,
+    outbox, inbox, early, wg, wg_rows, wg_deep, wg_full,
     local_sem, tile_sem, out_sem, gather_send, gather_recv, halo_send, halo_recv,
     s1, s2, s3, r1, r2, r3,
 ):
@@ -96,6 +97,7 @@
     first_sel = dot(first, sel[...])
     state[0, 0:c, 0:n] = first.astype(F32)
     state[0, 0:c, n:wide] = first_sel
+    cotx[my_rows, n:wide] = first_sel.astype(BF16)
     state[0, c:, :] = jnp.zeros((c, wide), F32)
     state[1] = jnp.zeros((2 * c, wide), F32)
     parts[...] = jnp.zeros(parts.shape, BF16)
@@ -109,17 +111,18 @@
             outbox.at[parity, s], inbox.at[parity, s], halo_send.at[parity, s], halo_recv.at[parity, s], halo_to[s]
         )
 
+    def gathered(which, x):
+        rows = pl.ds(pl.multiple_of(x * c, c), c)
+        return (cotx.at[rows, pl.ds(n, halo)], cotx.at[rows, pl.ds(0, n)], feat.at[rows, :])[which]
+
     def gather_copy(which, j):
-        src = (cot_hbm, feat_hbm)[which]
-        dst = (own_cot, own_feat)[which]
-        return remote(src, dst, gather_send.at[which, j], gather_recv.at[which, xc], {"chan": chan_of[j]})
+        block = gathered(which, xc)
+        return remote(block, block, gather_send.at[which, j], gather_recv.at[which, xc], {"chan": chan_of[j]})
 
     def gather_wait(which):
         for x in chan_of:
-            rows = pl.ds(pl.multiple_of(x * c, c), c)
-            dst = (cotx.at[rows, pl.ds(0, n)], feat.at[rows, :])[which]
-            src = (cot_hbm, feat_hbm)[which]
-            remote(src, dst, gather_send.at[which, 0], gather_recv.at[which, x], {"chan": x}).wait_recv()
+            block = gathered(which, x)
+            remote(block, block, gather_send.at[which, 0], gather_recv.at[which, x], {"chan": x}).wait_recv()
 
     pl.semaphore_wait(barrier, len(greeted))
     for s in range(SLOTS):
@@ -130,36 +133,33 @@
 
     in_copies[2].wait()
 
+    sums[per_row] = jnp.zeros((tile, tile), F32)
+
     def assemble(r, carry):
         tile_copy(r).wait()
         columns = pl.ds(pl.multiple_of(r * tile, tile), tile)
-        marks = [cols[0, r, j] for j in range(per_row)]
-
-        def block(cb, carry):
-            total = jnp.zeros((tile, tile), F32)
+        block_of = [cols[0, r, j] for j in range(per_row)]
+        for j in range(per_row):
+            before = per_row
+            for i in range(j):
+                before = jnp.where(block_of[i] == block_of[j], i, before)
+            mine = tiles[r * per_row + j]
+            sums[j] = mine if j == 0 else mine + sums[before]
+        for cb in range(blocks + SLOTS):
+            last = per_row
             for j in range(per_row):
-                total += jnp.where(marks[j] == cb, 1.0, 0.0) * tiles[r * per_row + j]
-            hi, lo = split(total)
-            rows = pl.ds(pl.multiple_of(cb * tile, tile), tile)
-            e_hi[rows, columns] = hi
-            e_lo[rows, columns] = lo
-            return carry
-
-        return lax.fori_loop(0, blocks + SLOTS, block, carry)
+                last = jnp.where(block_of[j] == cb, j, last)
+            hi, lo = split(sums[last])
+            e_hi[cb * tile : (cb + 1) * tile, columns] = hi
+            e_lo[cb * tile : (cb + 1) * tile, columns] = lo
+        return carry
 
     lax.fori_loop(0, blocks, assemble, 0)
 
-    def extend(i, carry):
-        rows = pl.ds(pl.multiple_of(i * 2 * tile, 2 * tile), 2 * tile)
-        e_hi[rows, n:wide] = dot(e_hi[rows, 0:n], sel[...]).astype(BF16)
-        e_lo[rows, n:wide] = dot(e_lo[rows, 0:n], sel[...]).astype(BF16)
-        return carry
-
-    lax.fori_loop(0, wide // (2 * tile), extend, 0)
-
-    in_copies[3].wait()
-    gather_wait(0)
-    cotx[:, n:wide] = dot(cotx[:, 0:n], sel[...]).astype(BF16)
+    for e in (e_hi, e_lo):
+        for i in range(SLOTS // 2):
+            at = slice(2 * i * tile, 2 * (i + 1) * tile)
+            e[:, n + 2 * i * tile : n + 2 * (i + 1) * tile] = dot(e[:, 0:n], sel[:, at]).astype(BF16)
 
     chunk = halo
 
@@ -169,7 +169,9 @@
             full = dot(parts[...], e_hi[0:n, at])
             part = full[0 : 2 * c] + full[2 * c :] + dot(parts[0 : 2 * c], e_lo[0:n, at])
             base[0:c, at] = fac_u * part[0:c] - state[older, 0:c, at]
-            base[c:, at] = fac_b * part[c:] + dot(w[order], cotx[:, at]) - state[older, c:, at]
+            base[c:, at] = fac_b * part[c:] - state[older, c:, at]
+            if order is not None:
+                base[c:, at] += dot(w[order], cotx[:, at])
 
     def arrived(lhs, at):
         full = dot(lhs, e_hi[n:wide, at])
@@ -183,51 +185,65 @@
     def row_part(b):
         return pl.ds(pl.multiple_of(b * share, share), share)
 
-    def step1(k, j, sem_of):
-        return remote(wg.at[k, row_part(row_of[j])], wg_rows.at[k, sem_of], s1.at[j], r1.at[k, sem_of], row_to[j])
-
-    def step2(k, j, sem_of):
-        return remote(wg_deep.at[k, sem_of], wg_deep.at[k, sem_of], s2.at[j], r2.at[k, sem_of], deep_to[j])
-
-    def step3(k, j, sem_of):
-        part = wg_full.at[k, row_part(sem_of)]
-        return remote(part, part, s3.at[j], r3.at[k, sem_of], row_to[j])
-
-    def send_rows(k, again):
+    def orders_of(i):
+        low, high = BATCHES[i]
+        return pl.ds(low, high - low)
+
+    def step1(i, j, sem_of):
+        k = orders_of(i)
+        return remote(wg.at[k, row_part(row_of[j])], wg_rows.at[sem_of, k], s1.at[i, j], r1.at[i, sem_of], row_to[j])
+
+    def step2(i, j, sem_of):
+        part = wg_deep.at[sem_of, orders_of(i)]
+        return remote(part, part, s2.at[i, j], r2.at[i, sem_of], deep_to[j])
+
+    def step3(i, j, sem_of):
+        part = wg_full.at[orders_of(i), row_part(sem_of)]
+        return remote(part, part, s3.at[i, j], r3.at[i, sem_of], row_to[j])
+
+    def send_rows(i):
+        k = orders_of(i)
         for j in range(group - 1):
-            if again:
-                step1(k, j, bc).wait_send()
-        wg_rows[k, bc] = wg[k, row_part(bc), :]
+            step1(i, j, bc).start()
+        wg_rows[bc, k] = wg[k, row_part(bc), :]
+
+    def send_deep(i):
+        k = orders_of(i)
         for j in range(group - 1):
-            step1(k, j, bc).start()
-
-    def send_deep(k, again):
-        for j in range(group - 1):
-            step1(k, j, row_of[j]).wait_recv()
+            step1(i, j, row_of[j]).wait_recv()
+        total = wg_rows[0, k]
+        for j in range(1, group):
+            total += wg_rows[j, k]
+        wg_deep[zc, k] = total
         for j in range(depth - 1):
-            if again:
-                step2(k, j, zc).wait_send()
-        total = wg_rows[k, 0]
-        for j in range(1, group):
-            total += wg_rows[k, j]
-        wg_deep[k, zc] = total
+            step2(i, j, zc).start()
+
+    def send_back(i):
+        k = orders_of(i)
         for j in range(depth - 1):
-            step2(k, j, zc).start()
-
-    def send_back(k, again):
-        for j in range(depth - 1):
-            step2(k, j, deep_of[j]).wait_recv()
-        for j in range(group - 1):
-            if again:
-                step3(k, j, bc).wait_send()
-        total = wg_deep[k, 0]
+            step2(i, j, deep_of[j]).wait_recv()
+        total = wg_deep[0, k]
         for j in range(1, depth):
-            total += wg_deep[k, j]
+            total += wg_deep[j, k]
         wg_full[k, row_part(bc), :] = total * scale
         for j in range(group - 1):
-            step3(k, j, bc).start()
-
-    prepare(top, 1.0, 2.0, 1)
+            step3(i, j, bc).start()
+
+    def at_round(r, when, step, among=range(len(BATCHES))):
+        for i in among:
+            if when(BATCHES[i][1]) < top:
+                pl.when(r == when(BATCHES[i][1]))(functools.partial(step, i))
+
+    def deep_round(high):
+        return high - 1
+
+    def back_round(high):
+        return high + 1 if high < top - 1 else high
+
+    prepare(None, 1.0, 2.0, 1)
+    in_copies[3].wait()
+    gather_wait(0)
+    base[c:, n:wide] += dot(w[top], cotx[:, n:wide])
 
     def round_(r, carry):
         parity = lax.rem(r, 2)
@@ -254,6 +270,15 @@
                 outbox[other, s, i * c : (i + 1) * c] = piece[:, cut]
         for s in range(SLOTS):
             halo_copy(other, s).start()
+
+        @pl.when(r == 0)
+        def _():
+            gather_wait(1)
+            in_copies[4].wait()
+            for j in range(chan - 1):
+                gather_copy(2, j).start()
+            base[c:, 0:n] += dot(w[top], cotx[:, 0:n])
+
         for i in range(n // chunk):
             at = slice(i * chunk, (i + 1) * chunk)
             got = arrived(lhs, at)
@@ -265,39 +290,41 @@
                 row = (0, 2, 1, 3)[j] * c
                 parts[row : row + c, at] = piece
 
+        def now():
+            return jnp.concatenate([parts[0:c], parts[2 * c : 3 * c]], axis=0)
+
+        def weigh(k, field):
+            both = dot_nt(field, feat[...])
+            wg[k] = both[0:c] + both[c:]
+
         @pl.when(r == 0)
         def _():
-            in_copies[4].wait()
-            gather_wait(1)
-            wg[0] = dot_nt(cotx[my_rows, 0:n], feat[...])
-            send_rows(0, False)
-
-        both = dot_nt(jnp.concatenate([parts[0:c], parts[2 * c : 3 * c]], axis=0), feat[...])
-        wg[r + 1] = both[0:c] + both[c:]
+            early[...] = now()
+
+        @pl.when(r > 1)
+        def _():
+            weigh(r + 1, now())
+
+        at_round(r, lambda high: high - 2, send_rows, range(1, len(BATCHES)))
         prepare(top - 1 - r, 2.0, jnp.where(r == top - 1, 1.0, 2.0).astype(F32), parity)
-
-        @pl.when(r == 2)
-        def _():
-            send_back(0, False)
-
-        @pl.when(r >= 2)
-        def _():
-            send_back(r - 1, True)
 
         @pl.when(r == 1)
         def _():
-            send_deep(0, False)
-
-        @pl.when(r >= 1)
-        def _():
-            send_deep(r, True)
-
-        send_rows(r + 1, True)
+            gather_wait(2)
+            wg[0] = dot_nt(cotx[my_rows, 0:n], feat[...])
+            weigh(1, early[...])
+            weigh(2, now())
+            send_rows(0)
+
+        at_round(r, back_round, send_back)
+        at_round(r, deep_round, send_deep)
         return carry
 
     lax.fori_loop(0, top, round_, 0)
 
-    send_deep(top, True)
+    for i, (_, high) in enumerate(BATCHES):
+        if deep_round(high) >= top:
+            send_deep(i)
     last = top % 2
     lhs = halo_in(last)
     for i in range(n // chunk):
@@ -305,35 +332,33 @@
         base[c:, at] = base[c:, at] + arrived(lhs, at)[c:]
     grad_copy = pltpu.make_async_copy(base.at[pl.ds(c, c), pl.ds(0, n)], grad_out, out_sem.at[0])
     grad_copy.start()
-    send_back(top - 1, True)
-    for k in range(top):
+    for i, (_, high) in enumerate(BATCHES):
+        if back_round(high) >= top:
+            send_back(i)
+    for i in range(len(BATCHES)):
         for j in range(group - 1):
-            step3(k, j, row_of[j]).wait_recv()
-    early = pltpu.make_async_copy(wg_full.at[pl.ds(0, top)], wg_out.at[pl.ds(0, top)], out_sem.at[1])
-    early.start()
-    send_back(top, True)
-    for j in range(group - 1):
-        step3(top, j, row_of[j]).wait_recv()
-    late = pltpu.make_async_copy(wg_full.at[top], wg_out.at[top], out_sem.at[2])
-    late.start()
-
-    for which in range(2):
+            step3(i, j, row_of[j]).wait_recv()
+    wg_copy = pltpu.make_async_copy(wg_full, wg_out, out_sem.at[1])
+    wg_copy.start()
+
+    for which in range(3):
         for j in range(chan - 1):
             gather_copy(which, j).wait_send()
     for parity in range(2):
         for s in range(SLOTS):
             halo_copy(parity, s).wait_send()
-    for j in range(group - 1):
-        step1(top, j, bc).wait_send()
-        step3(top, j, bc).wait_send()
-    for j in range(depth - 1):
-        step2(top, j, zc).wait_send()
+    for i in range(len(BATCHES)):
+        for j in range(group - 1):
+            step1(i, j, bc).wait_send()
+            step3(i, j, bc).wait_send()
+        for j in range(depth - 1):
+            step2(i, j, zc).wait_send()
     grad_copy.wait()
-    early.wait()
-    late.wait()
-
-
-def local(dom, chan, group, features, cotangent, weights, tile_values, tile_cols, send_list):
+    wg_copy.wait()
+
+
+def local(dom, chan, group, *arrays):
+    features, _, weights, tile_values, tile_cols, send_list = arrays
     c, n = features.shape
     orders, _, all_c = weights.shape
     tiles, tile, _ = tile_values.shape
@@ -356,6 +381,7 @@
             vmem((all_c, wide), BF16),
             vmem(weights.shape, BF16),
             vmem(tile_values.shape, F32),
+            vmem((tile_cols.shape[-1] + 1, tile, tile), F32),
             pltpu.SMEM(tile_cols.shape, jnp.int32),
             vmem(send_list.shape, jnp.int32),
             vmem((n, halo), BF16),
@@ -366,29 +392,26 @@
             vmem((2 * c, wide), F32),
             vmem((2, SLOTS, 4 * c, tile), BF16),
             vmem((2, SLOTS, 4 * c, tile), BF16),
+            vmem((2 * c, n), BF16),
             vmem((orders, c, all_c), F32),
-            vmem((orders, group, share, all_c), F32),
-            vmem((orders, depth, share, all_c), F32),
+            vmem((group, orders, share, all_c), F32),
+            vmem((depth, orders, share, all_c), F32),
             vmem((orders, c, all_c), F32),
             dma((5,)),
             dma((n // tile,)),
-            dma((3,)),
-            dma((2, chan)),
-            dma((2, chan)),
+            dma((2,)),
+            dma((3, chan)),
+            dma((3, chan)),
             dma((2, SLOTS)),
             dma((2, SLOTS)),
-            dma((group,)),
-            dma((depth,)),
-            dma((group,)),
-            dma((orders, group)),
-            dma((orders, depth)),
-            dma((orders, group)),
+            *[dma((len(BATCHES), k)) for k in (group, depth, group)],
+            *[dma((len(BATCHES), k)) for k in (group, depth, group)],
         ],
         compiler_params=pltpu.CompilerParams(
             collective_id=0, has_side_effects=True, vmem_limit_bytes=48 << 20
         ),
         name="clenshaw",
-    )(features, cotangent, weights, tile_values, tile_cols, send_list)
+    )(*(pltpu.with_memory_space_constraint(x, pltpu.HBM) for x in arrays))
     return input_grad, jnp.swapaxes(weight_grad, 1, 2)
 
 

time: 92.7 us -> 82.6 us (0.89)
  local copies, waits for them, and re-layouts: 7.84 us -> 1.52 us
  Pallas kernels: 83.9 us -> 80.1 us
    unnamed x14 -> x2, local copies, waits for them, and re-layouts: 7.84 us -> 1.52 us
    pallas_call x1, Pallas kernels: 83.9 us -> 80.1 us  [local(): pl.pallas_call(functools.partial(kernel, (dom, chan, group, scale)), out_...]
where the time goes in v2:
time: 82.6 us; the launch traced here: 82.3 us
  Pallas kernels  80.1 us (97%)
  local copies, waits for them, and re-layouts  1.52 us (2%)
    pallas_call x1, Pallas kernels, local(): pl.pallas_call(functools.partial(kernel, (dom, chan, group, scale)), out_...  80.1 us

profile of v2, /device:TPU:1, one launch (start us, length us, event | category | flops | bytes accessed | tf_op | source)
XLA Modules:
  0.0 82.3 jit_solution(8527352189312570943)
XLA Ops:
  0.6 80.1 %clenshaw.1 = (f32[64,1024]{1,0:T(8,128)S(1)}, f32[9,64,256]{2,1,0:T(8,128)S(1)}) custom-call(bf16[64,1024]{1,0:T(8,128)(2,1)} %feat_hbm.1, bf16[64,1024]{1,0:T(8,128)(2,1)} %cot_hbm.1, bf16[9,64,256]{2,1,0:T(8,128)(2,1)} %w_hbm.1, f32[64,128,128]{2,1,0:T(8,128)} %tiles_hbm.1, s32[1,8,8]{2,1,0:T(8,128)} %cols_hbm.1, s32[1,4,128]{2,1,0:T(4,128)} %send_hbm.1), custom_call_target="tpu_custom_call" | custom-call | tf_op jit(solution)/shard_map/clenshaw/pallas_call | solution.py:371
  80.7 0.7 copy.10
  81.4 0.8 copy.11

commit v3 on v2

--- a/solution.py
+++ b/solution.py
@@ -10,7 +10,9 @@
 NEIGHBOUR_SHIFTS = (1, -1, 2, -2)
 SLOTS = len(NEIGHBOUR_SHIFTS)
 MESH = pl.DeviceIdType.MESH
-BATCHES = ((0, 3), (3, 6), (6, 7), (7, 8), (8, 9))
+LAST, AFTER = 8, 9
+BATCHES = ((0, 3, 1, 3, 5), (3, 5, 3, 4, 6), (5, 7, 5, 6, LAST), (7, 9, 6, 7, AFTER))
+ADJOINT = (2, 3, 3, 4)
 F32, BF16 = jnp.float32, jnp.bfloat16
 
 
@@ -32,8 +34,8 @@
     feat_hbm, cot_hbm, w_hbm, tiles_hbm, cols_hbm, send_hbm,
     grad_out, wg_out,
     feat, cotx, w, tiles, sums, cols, send, sel, e_hi, e_lo, state, parts, base,
-    outbox, inbox, early, wg, wg_rows, wg_deep, wg_full,
-    local_sem, tile_sem, out_sem, gather_send, gather_recv, halo_send, halo_recv,
+    outbox, inbox, early, f_out, f_in, f_own, f_hi, f_lo, wg, wg_rows, wg_deep, wg_full,
+    local_sem, tile_sem, out_sem, gather_send, gather_recv, halo_send, halo_recv, f_send, f_recv,
     s1, s2, s3, r1, r2, r3,
 ):
     dom, chan, group, scale = dims
@@ -48,6 +50,7 @@
     wide = n + halo
     per_row = tiles.shape[0] // blocks
     share = c // group
+    all_c = feat.shape[0]
 
     def along_dom(index):
         return {"dom": index}
@@ -124,13 +127,6 @@
             block = gathered(which, x)
             remote(block, block, gather_send.at[which, 0], gather_recv.at[which, x], {"chan": x}).wait_recv()
 
-    pl.semaphore_wait(barrier, len(greeted))
-    for s in range(SLOTS):
-        halo_copy(0, s).start()
-    for which in range(2):
-        for j in range(chan - 1):
-            gather_copy(which, j).start()
-
     in_copies[2].wait()
 
     sums[per_row] = jnp.zeros((tile, tile), F32)
@@ -156,6 +152,13 @@
 
     lax.fori_loop(0, blocks, assemble, 0)
 
+    pl.semaphore_wait(barrier, len(greeted))
+    for s in range(SLOTS):
+        halo_copy(0, s).start()
+    for which in range(2):
+        for j in range(chan - 1):
+            gather_copy(which, j).start()
+
     for e in (e_hi, e_lo):
         for i in range(SLOTS // 2):
             at = slice(2 * i * tile, 2 * (i + 1) * tile)
@@ -186,7 +189,7 @@
         return pl.ds(pl.multiple_of(b * share, share), share)
 
     def orders_of(i):
-        low, high = BATCHES[i]
+        low, high = BATCHES[i][:2]
         return pl.ds(low, high - low)
 
     def step1(i, j, sem_of):
@@ -229,16 +232,39 @@
         for j in range(group - 1):
             step3(i, j, bc).start()
 
-    def at_round(r, when, step, among=range(len(BATCHES))):
+    def at_round(r, column, step, among=range(len(BATCHES))):
         for i in among:
-            if when(BATCHES[i][1]) < top:
-                pl.when(r == when(BATCHES[i][1]))(functools.partial(step, i))
-
-    def deep_round(high):
-        return high - 1
-
-    def back_round(high):
-        return high + 1 if high < top - 1 else high
+            if BATCHES[i][column] < top:
+                pl.when(r == BATCHES[i][column])(functools.partial(step, i))
+
+    def adjoint_copy(s):
+        to = along_dom(lax.rem(me - NEIGHBOUR_SHIFTS[s] + dom, dom))
+        return remote(f_out.at[s], f_in.at[s], f_send.at[s], f_recv.at[s], to)
+
+    def adjoint_rows(rows):
+        return dot_nt(e_hi[rows, 0:n], feat[...]) + dot_nt(e_lo[rows, 0:n], feat[...])
+
+    def adjoint_out():
+        hi, lo = split(adjoint_rows(slice(n, wide)))
+        for s in range(SLOTS):
+            rows = slice(s * tile, (s + 1) * tile)
+            f_out[s, :, 0:all_c] = hi[rows]
+            f_out[s, :, all_c:] = lo[rows]
+
+    def adjoint_send():
+        for s in range(SLOTS):
+            adjoint_copy(s).start()
+
+    def adjoint_own():
+        f_own[...] = adjoint_rows(slice(0, n))
+
+    def adjoint_in():
+        for s in range(SLOTS):
+            adjoint_copy(s).wait_recv()
+        both = dot(sel[...], f_in[...].reshape(halo, 2 * all_c))
+        hi, lo = split(f_own[...] + both[:, 0:all_c] + both[:, all_c:])
+        f_hi[...] = hi
+        f_lo[...] = lo
 
     prepare(None, 1.0, 2.0, 1)
     in_copies[3].wait()
@@ -279,6 +305,10 @@
                 gather_copy(2, j).start()
             base[c:, 0:n] += dot(w[top], cotx[:, 0:n])
 
+        pl.when(r == ADJOINT[1])(adjoint_send)
+        at_round(r, 3, send_deep)
+        at_round(r, 4, send_back)
+
         for i in range(n // chunk):
             at = slice(i * chunk, (i + 1) * chunk)
             got = arrived(lhs, at)
@@ -301,11 +331,17 @@
         def _():
             early[...] = now()
 
-        @pl.when(r > 1)
+        @pl.when(jnp.logical_and(r > 1, r < top - 1))
         def _():
             weigh(r + 1, now())
 
-        at_round(r, lambda high: high - 2, send_rows, range(1, len(BATCHES)))
+        @pl.when(r == top - 2)
+        def _():
+            both = dot(now(), f_hi[...])
+            twice = both[0:c] + both[c:] + dot(parts[0:c], f_lo[...])
+            wg[top] = 2.0 * twice - wg[top - 2]
+
+        at_round(r, 2, send_rows, range(1, len(BATCHES)))
         prepare(top - 1 - r, 2.0, jnp.where(r == top - 1, 1.0, 2.0).astype(F32), parity)
 
         @pl.when(r == 1)
@@ -316,15 +352,18 @@
             weigh(2, now())
             send_rows(0)
 
-        at_round(r, back_round, send_back)
-        at_round(r, deep_round, send_deep)
+        for at, step in zip(ADJOINT[::2] + ADJOINT[3:], (adjoint_out, adjoint_own, adjoint_in)):
+            pl.when(r == at)(step)
         return carry
 
     lax.fori_loop(0, top, round_, 0)
 
-    for i, (_, high) in enumerate(BATCHES):
-        if deep_round(high) >= top:
-            send_deep(i)
+    def send_back_at(place):
+        for i in range(len(BATCHES)):
+            if BATCHES[i][4] == place:
+                send_back(i)
+
+    send_back_at(LAST)
     last = top % 2
     lhs = halo_in(last)
     for i in range(n // chunk):
@@ -332,9 +371,7 @@
         base[c:, at] = base[c:, at] + arrived(lhs, at)[c:]
     grad_copy = pltpu.make_async_copy(base.at[pl.ds(c, c), pl.ds(0, n)], grad_out, out_sem.at[0])
     grad_copy.start()
-    for i, (_, high) in enumerate(BATCHES):
-        if back_round(high) >= top:
-            send_back(i)
+    send_back_at(AFTER)
     for i in range(len(BATCHES)):
         for j in range(group - 1):
             step3(i, j, row_of[j]).wait_recv()
@@ -353,6 +390,8 @@
             step3(i, j, bc).wait_send()
         for j in range(depth - 1):
             step2(i, j, zc).wait_send()
+    for s in range(SLOTS):
+        adjoint_copy(s).wait_send()
     grad_copy.wait()
     wg_copy.wait()
 
@@ -393,6 +432,11 @@
             vmem((2, SLOTS, 4 * c, tile), BF16),
             vmem((2, SLOTS, 4 * c, tile), BF16),
             vmem((2 * c, n), BF16),
+            vmem((SLOTS, tile, 2 * all_c), BF16),
+            vmem((SLOTS, tile, 2 * all_c), BF16),
+            vmem((n, all_c), F32),
+            vmem((n, all_c), BF16),
+            vmem((n, all_c), BF16),
             vmem((orders, c, all_c), F32),
             vmem((group, orders, share, all_c), F32),
             vmem((depth, orders, share, all_c), F32),
@@ -404,6 +448,8 @@
             dma((3, chan)),
             dma((2, SLOTS)),
             dma((2, SLOTS)),
+            dma((SLOTS,)),
+            dma((SLOTS,)),
             *[dma((len(BATCHES), k)) for k in (group, depth, group)],
             *[dma((len(BATCHES), k)) for k in (group, depth, group)],
         ],

time: 82.6 us -> 81.5 us (0.987)
  Pallas kernels: 80.1 us -> 79.1 us
    pallas_call x1, Pallas kernels: 80.1 us -> 79.1 us  [local(): pl.pallas_call(functools.partial(kernel, (dom, chan, group, scale)), out_...]
where the time goes in v3:
time: 81.5 us; the launch traced here: 81.3 us
  Pallas kernels  79.1 us (97%)
  local copies, waits for them, and re-layouts  1.52 us (2%)
    pallas_call x1, Pallas kernels, local(): pl.pallas_call(functools.partial(kernel, (dom, chan, group, scale)), out_...  79.1 us

profile of v3, /device:TPU:1, one launch (start us, length us, event | category | flops | bytes accessed | tf_op | source)
XLA Modules:
  0.0 81.3 jit_solution(12191791987416810758)
XLA Ops:
  0.6 79.1 %clenshaw.1 = (f32[64,1024]{1,0:T(8,128)S(1)}, f32[9,64,256]{2,1,0:T(8,128)S(1)}) custom-call(bf16[64,1024]{1,0:T(8,128)(2,1)} %feat_hbm.1, bf16[64,1024]{1,0:T(8,128)(2,1)} %cot_hbm.1, bf16[9,64,256]{2,1,0:T(8,128)(2,1)} %w_hbm.1, f32[64,128,128]{2,1,0:T(8,128)} %tiles_hbm.1, s32[1,8,8]{2,1,0:T(8,128)} %cols_hbm.1, s32[1,4,128]{2,1,0:T(4,128)} %send_hbm.1), custom_call_target="tpu_custom_call" | custom-call | tf_op jit(solution)/shard_map/clenshaw/pallas_call | solution.py:410
  79.7 0.7 copy.10
  80.5 0.8 %copy.11 = f32[9,256,64]{1,2,0:T(8,128)} copy(f32[9,256,64]{1,2,0:T(8,128)S(1)} %bitcast.1) | data formatting | bytes 1179648

commit v4 on v3

--- a/solution.py
+++ b/solution.py
@@ -11,8 +11,8 @@
 SLOTS = len(NEIGHBOUR_SHIFTS)
 MESH = pl.DeviceIdType.MESH
 LAST, AFTER = 8, 9
-BATCHES = ((0, 3, 1, 3, 5), (3, 5, 3, 4, 6), (5, 7, 5, 6, LAST), (7, 9, 6, 7, AFTER))
-ADJOINT = (2, 3, 3, 4)
+BATCHES = ((0, 3, 1, 4, 6), (3, 5, 3, 5, 7), (5, 7, 5, 6, LAST), (7, 9, 6, 7, AFTER))
+ADJOINT = (2, 3, 2, 4)
 F32, BF16 = jnp.float32, jnp.bfloat16
 
 

time: 81.5 us -> 78.8 us (0.967)
  Pallas kernels: 79.1 us -> 76.6 us
    pallas_call x1, Pallas kernels: 79.1 us -> 76.6 us  [local(): pl.pallas_call(functools.partial(kernel, (dom, chan, group, scale)), out_...]
where the time goes in v4:
time: 78.8 us; the launch traced here: 78.7 us
  Pallas kernels  76.6 us (97%)
  local copies, waits for them, and re-layouts  1.52 us (2%)
    pallas_call x1, Pallas kernels, local(): pl.pallas_call(functools.partial(kernel, (dom, chan, group, scale)), out_...  76.6 us

profile of v4, /device:TPU:1, one launch (start us, length us, event | category | flops | bytes accessed | tf_op | source)
XLA Modules:
  0.0 78.7 jit_solution(13375730819855124092)
XLA Ops:
  0.6 76.6 %clenshaw.1 = (f32[64,1024]{1,0:T(8,128)S(1)}, f32[9,64,256]{2,1,0:T(8,128)S(1)}) custom-call(bf16[64,1024]{1,0:T(8,128)(2,1)} %feat_hbm.1, bf16[64,1024]{1,0:T(8,128)(2,1)} %cot_hbm.1, bf16[9,64,256]{2,1,0:T(8,128)(2,1)} %w_hbm.1, f32[64,128,128]{2,1,0:T(8,128)} %tiles_hbm.1, s32[1,8,8]{2,1,0:T(8,128)} %cols_hbm.1, s32[1,4,128]{2,1,0:T(4,128)} %send_hbm.1), custom_call_target="tpu_custom_call" | custom-call | tf_op jit(solution)/shard_map/clenshaw/pallas_call | solution.py:410
  77.2 0.7 copy.10
  77.9 0.8 %copy.11 = f32[9,256,64]{1,2,0:T(8,128)} copy(f32[9,256,64]{1,2,0:T(8,128)S(1)} %bitcast.1) | data formatting | bytes 1179648

commit v5 on v4

--- a/solution.py
+++ b/solution.py
@@ -306,8 +306,9 @@
             base[c:, 0:n] += dot(w[top], cotx[:, 0:n])
 
         pl.when(r == ADJOINT[1])(adjoint_send)
-        at_round(r, 3, send_deep)
-        at_round(r, 4, send_back)
+        busy = top - 2
+        for column, step in ((3, send_deep), (4, send_back)):
+            at_round(r, column, step, [i for i in range(len(BATCHES)) if BATCHES[i][column] != busy])
 
         for i in range(n // chunk):
             at = slice(i * chunk, (i + 1) * chunk)
@@ -342,6 +343,8 @@
             wg[top] = 2.0 * twice - wg[top - 2]
 
         at_round(r, 2, send_rows, range(1, len(BATCHES)))
+        for column, step in ((3, send_deep), (4, send_back)):
+            at_round(r, column, step, [i for i in range(len(BATCHES)) if BATCHES[i][column] == busy])
         prepare(top - 1 - r, 2.0, jnp.where(r == top - 1, 1.0, 2.0).astype(F32), parity)
 
         @pl.when(r == 1)

time: 78.8 us -> 78.3 us (level)
  no operation moved by 1% of the time
where the time goes in v5:
time: 78.3 us
  Pallas kernels  76.1 us (97%)
  local copies, waits for them, and re-layouts  1.52 us (2%)
    pallas_call x1, Pallas kernels, local(): pl.pallas_call(functools.partial(kernel, (dom, chan, group, scale)), out_...  76.1 us

profile of v5, /device:TPU:1, one launch (start us, length us, event | category | flops | bytes accessed | tf_op | source)
XLA Modules:
  0.0 78.3 jit_solution(8067629947950106161)
XLA Ops:
  0.6 76.1 %clenshaw.1 = (f32[64,1024]{1,0:T(8,128)S(1)}, f32[9,64,256]{2,1,0:T(8,128)S(1)}) custom-call(bf16[64,1024]{1,0:T(8,128)(2,1)} %feat_hbm.1, bf16[64,1024]{1,0:T(8,128)(2,1)} %cot_hbm.1, bf16[9,64,256]{2,1,0:T(8,128)(2,1)} %w_hbm.1, f32[64,128,128]{2,1,0:T(8,128)} %tiles_hbm.1, s32[1,8,8]{2,1,0:T(8,128)} %cols_hbm.1, s32[1,4,128]{2,1,0:T(4,128)} %send_hbm.1), custom_call_target="tpu_custom_call" | custom-call | tf_op jit(solution)/shard_map/clenshaw/pallas_call | solution.py:413
  76.7 0.7 copy.10
  77.4 0.8 %copy.11 = f32[9,256,64]{1,2,0:T(8,128)} copy(f32[9,256,64]{1,2,0:T(8,128)S(1)} %bitcast.1) | data formatting | bytes 1179648
